TPU v7x, 256 devices: a whole 4x4x8 slice. The times are simulated.
256 devices in a mesh: nest: 2 (over core), bin: 128 (over y, z, x).
Axes of the slice: x: 4, y: 4, z: 8, core: 2. Of those that a mesh axis runs over, the one named last changes fastest.
Arguments:
- spectra: float32 [2, 1152, 8192], P('nest', 'bin'), may hold values from 0.05 to 2
- courant: float32 [2, 1152], P(None, 'bin'), may hold values from -0.9 to 0.9
- coupling: bfloat16 [1152, 1152], replicated, may hold values from -0.1875 to 0.1875
- growth: float32 [1152], replicated, may hold values from 0.05 to 0.5
- dissipation: float32 [1152], replicated, may hold values from 0.2 to 2
- wind: float32 [2, 8192], P('nest'), may hold values from 0.5 to 2
- neighbours: int32 [2, 4, 8192], P('nest'), may hold values from 0 to 8191, as said below
- wet_mask: int32 [2, 8192], P('nest'), may hold values from 0 to 1, as said below
- send_list: int32 [2, 2048], P('nest'), may hold values from 0 to 8191, as said below
- recv_list: int32 [2, 2048], P('nest'), may hold values from 0 to 8191, as said below
- substep_count: int32 [2], P('nest'), may hold values from 1 to 2, as said below
Outputs:
- new_spectra: float32 [2, 1152, 8192], P('nest', 'bin')
Inputs may be any that keep to these rules, and one draw needn't show every extreme that they name: `neighbours`: row 0 holds each point's east neighbour, row 1 west, row 2 north, row 3 south, on a periodic grid of 32 rows of 256 points; grid row r holds the point numbers r * 256 to (r + 1) * 256 - 1 in some order. `wet_mask`: exactly 4096 points of each nest are sea points. `send_list`: distinct sea points of the nest, none of them in recv_list of the same nest. `recv_list`: distinct sea points of the nest. `substep_count`: some nest takes 2 substeps.
All inputs are finite; a program needn't handle non-finite values.
Results may differ from a plain program's by a relative error of at most 0.0012.
Values sent between devices are 32-bit elements; how exact they have to be, the bound alone decides.
A program may use at most 64 MiB of HBM per device.

v0:
```python
import jax
import jax.numpy as jnp
from jax import lax
from jax.sharding import PartitionSpec as P

SUBSTEPS = 2
SRC = 5


source_dt = 0.25
tiny_add = 1e-06


def from_partner(array, axis, stride):
    return lax.ppermute(array, axis, [(i, i ^ 1 << stride) for i in range(lax.axis_size(axis))])


def advect_grid(field, rate, axis_dim):
    magnitude = jnp.abs(rate)
    forward = rate >= 0.0
    next_cell = jnp.roll(field, -1, axis=axis_dim)
    prev_cell = jnp.roll(field, 1, axis=axis_dim)
    next_next = jnp.roll(field, -2, axis=axis_dim)
    upwind = jnp.where(forward, field, next_cell)
    downwind = jnp.where(forward, next_cell, field)
    far_upwind = jnp.where(forward, prev_cell, next_next)
    estimate = (
        0.5 * (upwind + downwind)
        - 0.5 * magnitude * (downwind - upwind)
        - (1.0 - magnitude * magnitude) / 6.0 * (downwind - 2.0 * upwind + far_upwind)
    )
    face_value = jnp.clip(estimate, jnp.minimum(upwind, downwind), jnp.maximum(upwind, downwind))
    return field - rate * (face_value - jnp.roll(face_value, 1, axis=axis_dim))


def integrate(columns, wind_cols, coupling, growth, dissipation):
    for repeat in range(SRC):
        linear = jnp.dot(coupling, columns.astype(jnp.bfloat16), preferred_element_type=jnp.float32)
        spread = jnp.sqrt(jnp.mean(columns * columns, axis=0) + tiny_add)
        columns = (
            columns + source_dt * (linear + growth[:, None] * wind_cols[None, :] * columns)
        ) / (1.0 + source_dt * dissipation[:, None] * spread[None, :])
    return columns


def grid_order(east_index, north_index, rows_count, cols_count):

    def north_walk(point, unused):
        return (north_index[point], point)

    def east_walk(point, unused):
        return (east_index[point], point)

    starts = lax.scan(north_walk, jnp.int32(0), None, length=rows_count)[1]
    walked = lax.scan(east_walk, starts, None, length=cols_count)[1]
    return walked.T.reshape(-1)


def local(
    spectra,
    courant,
    coupling,
    growth,
    dissipation,
    wind,
    neighbours,
    wet_mask,
    send_list,
    recv_list,
    substep_count,
):
    field = spectra[0]
    bins_here = field.shape[0]
    points = field.shape[1]
    cols_count = min(256, points // 4)
    rows_count = points // cols_count
    tables = neighbours[0]
    ordering = grid_order(tables[0], tables[2], rows_count, cols_count)
    position = jnp.zeros((points,), jnp.int32).at[ordering].set(jnp.arange(points, dtype=jnp.int32))
    sea_int = wet_mask[0]
    sea = sea_int.astype(jnp.float32)
    sea_grid = sea[ordering].reshape(1, rows_count, cols_count)
    steps_here = substep_count[0]
    rates = courant / steps_here.astype(jnp.float32)
    rate_east = rates[0][:, None, None]
    rate_north = rates[1][:, None, None]
    send_slots = position[send_list[0]]
    recv_slots = position[recv_list[0]]
    gridded = (field * sea[None, :])[:, ordering]
    for substep in range(SUBSTEPS):
        outgoing = gridded[:, send_slots]
        incoming = from_partner(outgoing, "nest", 0)
        current = gridded.at[:, recv_slots].set(incoming).reshape(bins_here, rows_count, cols_count)
        current = advect_grid(current, rate_east, 2)
        current = advect_grid(current, rate_north, 1)
        current = (current * sea_grid).reshape(bins_here, points)
        gridded = jnp.where(substep < steps_here, current, gridded)
    field = gridded[:, position]
    devices = lax.axis_size("bin")
    my_rank = lax.axis_index("bin")
    wind_here = wind[0]
    columns = lax.all_to_all(field, "bin", split_axis=1, concat_axis=0, tiled=True)
    share = points // devices
    wind_cols = lax.dynamic_slice_in_dim(wind_here, my_rank * share, share)
    columns = integrate(columns, wind_cols, coupling, growth, dissipation)
    returned = lax.all_to_all(columns, "bin", split_axis=0, concat_axis=1, tiled=True)
    result_field = returned * sea[None, :]
    return result_field[None]


def solution(mesh):
    in_specs = (
        P("nest", "bin", None),
        P(None, "bin"),
        P(),
        P(),
        P(),
        P("nest", None),
        P("nest", None, None),
        P("nest", None),
        P("nest", None),
        P("nest", None),
        P("nest"),
    )
    out_specs = P("nest", "bin", None)
    return jax.shard_map(local, mesh=mesh, in_specs=in_specs, out_specs=out_specs, check_vma=False)
```

profile of v0, /device:TPU:2, one launch (start us, length us, event | category | flops | bytes accessed | tf_op | source)
XLA Modules:
  0.0 584.6 jit_solution(6738188270955024505)
XLA Ops:
  0.0 1.2 fusion.36
  1.2 44.7 %while.24 = (s32[]{:T(128)}, s32[]{:T(128)}, s32[32]{0:T(128)S(1)}, s32[8192]{0:T(1024)S(1)}, s32[]{:T(128)}, /*index=5*/s32[]{:T(128)}, s32[]{:T(128)}) while((s32[]{:T(128)}, s32[]{:T(128)}, s32[32]{0:T(128)S(1)}, s32[8192]{0:T(1024)S(1)}, s32[]{:T(128)}, /*index=5*/s32[]{:T(128)}, s32[]{:T(128)}) %tuple.70), condition=%wide.region_1.2_spmd, body=%wide.region_0.1_spmd.sunk | while | flops 5 | bytes 143 | solution.py:54
  45.9 194.8 %while.25 = (s32[]{:T(128)}, s32[32]{0:T(128)S(1)}, s32[256,32]{1,0:T(8,128)S(1)}, s32[8192]{0:T(1024)S(1)}, s32[]{:T(128)}, /*index=5*/s32[]{:T(128)}) while((s32[]{:T(128)}, s32[32]{0:T(128)S(1)}, s32[256,32]{1,0:T(8,128)S(1)}, s32[8192]{0:T(1024)S(1)}, s32[]{:T(128)}, /*index=5*/s32[]{:T(128)}) %tuple.69), condition=%wide.region_3.4_spmd, body=%wide.region_2.3_spmd.sunk | while | flops 1122 | bytes 5193 | solution.py:55
  240.9 0.8 convert_element_type.26
  241.7 4.1 copy.69
  245.8 30.5 %scatter_custom_fusion = s32[8192]{0:T(1024)S(1)} fusion(s32[8192]{0:T(1024)S(1)} %bitcast.233, s32[8192]{0:T(1024)S(1)} %iota.3, s32[]{:T(128)} %constant.32.clone.1), kind=kCustom, calls=%fused_computation.87 | custom fusion | bytes 32772 | tf_op jit(solution)/shard_map/scatter | solution.py:79
  276.4 11.8 %gather_fusion.3 = s32[2048]{0:T(1024)S(1)} fusion(s32[8192]{0:T(1024)S(1)} %scatter_custom_fusion, s32[2048]{0:T(1024)S(1)} %broadcast_clamp_fusion.2), kind=kCustom, calls=%fused_computation.3 | custom fusion | bytes 24576 | tf_op jit(solution)/shard_map/gather | solution.py:87
  288.2 4.2 bitcast_multiply_fusion
  292.4 30.0 %gather_fusion.1 = f32[8192,9]{1,0:T(8,128)} fusion(f32[9,8192]{0,1:T(8,128)} %bitcast_multiply_fusion, s32[8192]{0:T(1024)S(1)} %broadcast_clamp_fusion), kind=kCustom, calls=%fused_computation.1 | custom fusion | bytes 622592 | tf_op jit(solution)/shard_map/gather | solution.py:89
  322.4 9.8 %gather_fusion.4 = f32[2048,9]{1,0:T(8,128)} fusion(f32[9,8192]{0,1:T(8,128)} %bitcast.183, s32[2048]{0:T(1024)S(1)} %broadcast_clamp_fusion.1), kind=kCustom, calls=%fused_computation.4 | custom fusion | bytes 155648 | tf_op jit(solution)/shard_map/gather | solution.py:91
  332.1 1.5 copy.73
  334.5 11.8 %gather_fusion.2 = s32[2048]{0:T(1024)S(1)} fusion(s32[8192]{0:T(1024)S(1)} %scatter_custom_fusion, s32[2048]{0:T(1024)S(1)} %broadcast_clamp_fusion.3), kind=kCustom, calls=%fused_computation.2 | custom fusion | bytes 24576 | tf_op jit(solution)/shard_map/gather | solution.py:88
  346.3 3.5 copy.71
  349.9 45.5 %gather_fusion.5 = f32[8192]{0:T(1024)S(1)} fusion(f32[8192]{0:T(1024)S(1)} %bitcast.180, s32[8192]{0:T(1024)S(1)} %broadcast_clamp_fusion), kind=kCustom, calls=%fused_computation.5 | custom fusion | bytes 98304 | tf_op jit(solution)/shard_map/gather | solution.py:82
  395.4 1.3 copy.75
  396.8 10.0 %scatter_fusion = f32[9,8192]{0,1:T(8,128)} fusion(f32[9,8192]{0,1:T(8,128)} %bitcast.184, s32[2048]{0:T(1024)S(1)} %bitcast.235, f32[2048,9]{1,0:T(8,128)} %copy.75), kind=kCustom, calls=%fused_computation.9 | custom fusion | bytes 229376 | tf_op jit(solution)/shard_map/scatter | solution.py:93
  406.8 2.9 copy.76
  410.1 1.2 maximum_minimum_fusion.3
  411.4 0.9 multiply_subtract_fusion.1
  412.2 0.9 fusion.33
  413.1 0.8 slice.186
  413.9 3.6 copy.86
  417.4 1.4 maximum_minimum_fusion.2
  422.0 0.8 bitcast_select_fusion
  422.8 2.6 copy.90
  425.4 9.8 %gather_fusion.6 = f32[2048,9]{1,0:T(8,128)} fusion(f32[9,8192]{0,1:T(8,128)} %copy.90, s32[2048]{0:T(1024)S(1)} %broadcast_clamp_fusion.1), kind=kCustom, calls=%fused_computation.6 | custom fusion | bytes 155648 | tf_op jit(solution)/shard_map/gather | solution.py:91
  435.2 1.5 copy.89
  437.3 1.0 collective-permute-done.1
  438.9 2.2 copy.91
  441.2 10.0 %scatter_fusion.1 = f32[9,8192]{0,1:T(8,128)} fusion(f32[9,8192]{0,1:T(8,128)} %copy.90, s32[2048]{0:T(1024)S(1)} %bitcast.236, f32[2048,9]{1,0:T(8,128)} %copy.91), kind=kCustom, calls=%fused_computation.10 | custom fusion | bytes 229376 | tf_op jit(solution)/shard_map/scatter | solution.py:93
  451.2 2.9 copy.92
  454.5 1.2 maximum_minimum_fusion.1
  455.8 0.9 multiply_subtract_fusion
  456.6 0.9 fusion.29
  457.6 3.6 copy.102
  461.1 1.3 maximum_minimum_fusion
  465.6 0.8 multiply_select_fusion
  466.4 2.7 copy.104
  469.1 29.9 %gather_fusion.7 = f32[8192,9]{1,0:T(8,128)} fusion(f32[9,8192]{0,1:T(8,128)} %copy.104, s32[8192]{0:T(1024)S(1)} %fusion.25), kind=kCustom, calls=%fused_computation.7 | custom fusion | bytes 622592 | tf_op jit(solution)/shard_map/gather | solution.py:98
  499.0 3.8 copy.105
  502.8 2.4 reshape.374
  505.2 15.6 %all-to-all-start = ((f32[128,1,576]{2,1,0:T(1,128)}), f32[128,1,576]{2,1,0:T(1,128)S(1)}, u32[]{:S(2)}, u32[]{:S(2)}) async-start(f32[128,1,576]{2,1,0:T(1,128)} %reshape.374), calls=%async_computation | async-start | bytes 655360 | tf_op jit(solution)/shard_map/all_to_all | solution.py:102
  521.5 14.8 %all-to-all-done = f32[128,1,576]{2,1,0:T(1,128)S(1)} async-done(((f32[128,1,576]{2,1,0:T(1,128)}), f32[128,1,576]{2,1,0:T(1,128)S(1)}, u32[]{:S(2)}, u32[]{:S(2)}) %all-to-all-start) | async-done | bytes 294944 | tf_op jit(solution)/shard_map/all_to_all | solution.py:102
  536.9 1.4 reduce.1
  538.3 1.2 reshape.375
  539.4 2.3 bitcast_bitcast_fusion
  541.7 1.5 multiply_reduce_fusion
  543.2 1.3 all_to_all.31
  544.5 0.9 copy.107
  545.4 2.0 multiply_reduce_fusion.4
  547.5 1.1 multiply_reduce_fusion.3
  548.6 1.1 multiply_reduce_fusion.2
  549.6 1.1 multiply_reduce_fusion.1
  550.7 1.7 fusion.3
  552.4 1.2 copy.108
  553.6 1.1 all_to_all.32
  554.6 1.7 reshape.376
  556.3 21.2 %all_to_all.38 = f32[128,1,576]{2,1,0:T(1,128)S(1)} all-to-all(f32[128,1,576]{2,1,0:T(1,128)S(1)} %reshape.376), channel_id=1, replica_groups=mesh['nest'=2,'bin'=128] {'bin'}, dimensions={0} | all-to-all | bytes 589824 | tf_op jit(solution)/shard_map/all_to_all | solution.py:106
  577.5 1.4 reduce.2
  578.9 1.2 reshape.377
  580.1 1.4 copy.109
  581.5 1.0 all_to_all.35
  582.5 1.1 broadcast_multiply_fusion
  583.6 1.0 copy.110
  (1209 shorter events, 224.4 us)
Async XLA Ops:
  0.0 545.4 %copy-start = (bf16[1152,1152]{1,0:T(8,128)(2,1)S(1)}, bf16[1152,1152]{1,0:T(8,128)(2,1)}, u32[]{:S(2)}) copy-start(bf16[1152,1152]{1,0:T(8,128)(2,1)} %param.17) | copy-start | bytes 7962628
  0.0 276.3 %copy-start.16 = (s32[1,2048]{1,0:T(1,128)S(1)}, s32[1,2048]{1,0:T(1,128)}, u32[]{:S(2)}) copy-start(s32[1,2048]{1,0:T(1,128)} %param.23) | copy-start | bytes 24580
  292.4 42.0 %copy-start.19 = (f32[2,9]{1,0:T(2,128)S(1)}, f32[2,9]{1,0:T(2,128)}, u32[]{:S(2)}) copy-start(f32[2,9]{1,0:T(2,128)} %param.16) | copy-start | bytes 220
  292.4 42.1 %copy-start.17 = (s32[1,2048]{1,0:T(1,128)S(1)}, s32[1,2048]{1,0:T(1,128)}, u32[]{:S(2)}) copy-start(s32[1,2048]{1,0:T(1,128)} %param.24) | copy-start | bytes 24580
  333.7 61.7 %collective-permute-start = (f32[9,2048]{1,0:T(8,128)S(1)}, f32[9,2048]{1,0:T(8,128)S(1)}, u32[]{:S(2)}, u32[]{:S(2)}) collective-permute-start(f32[9,2048]{1,0:T(8,128)S(1)} %copy.73), channel_id=1, source_target_pairs={{0,128},{128,0},{1,129},{129,1},{2,130},{130,2},{3,131},{131,3},{4... | collective-permute-start | bytes 221192 | tf_op jit(solution)/shard_map/ppermute | solution.py:15
  418.9 1.6 copy-start.12
  419.0 1.8 copy-start.10
  419.4 1.8 copy-start.8
  419.7 1.8 copy-start.6
  420.1 1.8 copy-start.3
  420.1 1.8 copy-start.5
  422.8 28.4 %copy-start.1 = (f32[9,8192]{1,0:T(8,128)}, f32[9,8192]{1,0:T(8,128)S(1)}, u32[]{:S(2)}) copy-start(f32[9,8192]{1,0:T(8,128)S(1)} %bitcast_select_fusion) | copy-start | bytes 884740
  436.7 1.6 collective-permute-start.1
  438.3 0.7 copy-start.14
  462.5 1.6 copy-start.13
  462.6 1.8 copy-start.11
  463.0 1.8 copy-start.9
  463.4 1.8 copy-start.7
  463.7 1.8 copy-start.2
  463.7 1.8 copy-start.4
  499.0 22.5 %copy-start.18 = (f32[1152]{0:T(1024)S(1)}, f32[1152]{0:T(1024)}, u32[]{:S(2)}) copy-start(f32[1152]{0:T(1024)} %param.19) | copy-start | bytes 13828
  505.2 40.2 %copy-start.15 = (f32[1152]{0:T(1024)S(1)}, f32[1152]{0:T(1024)}, u32[]{:S(2)}) copy-start(f32[1152]{0:T(1024)} %param.18) | copy-start | bytes 13828
  505.2 31.1 %all-to-all-start = ((f32[128,1,576]{2,1,0:T(1,128)}), f32[128,1,576]{2,1,0:T(1,128)S(1)}, u32[]{:S(2)}, u32[]{:S(2)}) async-start(f32[128,1,576]{2,1,0:T(1,128)} %reshape.374), calls=%async_computation | async-start | bytes 655360 | tf_op jit(solution)/shard_map/all_to_all | solution.py:102
where the time goes:
time: 586 us; the launch traced here: 585 us
  local copies, waits for them, and re-layouts  477 us (81%)
  loops' own time  24.8 us (4%)
  other arithmetic  21.4 us (4%)
  blocking collectives  21.2 us (4%)
  starting transfers between devices  16.2 us (3%)
  waiting for transfers between devices  15.7 us (3%)
  matrix products  6.86 us (1%)
    gather x256, local copies, waits for them, and re-layouts, east_walk(): return (east_index[point], point)  179 us
    gather x1, local copies, waits for them, and re-layouts, local(): sea_grid = sea[ordering].reshape(1, rows_count, cols_count)  45.5 us
    gather x2, local copies, waits for them, and re-layouts, local(): gridded = (field * sea[None, :])[:, ordering]  33.5 us
    scatter x1, local copies, waits for them, and re-layouts, local(): jnp.zeros((points,), jnp.int32).at[ordering]  30.5 us
    gather x1, local copies, waits for them, and re-layouts, local(): field = gridded[:, position]  29.9 us
    scatter x4, local copies, waits for them, and re-layouts, local(): gridded.at[:, recv_slots].set(incoming)  27.2 us
    gather x4, local copies, waits for them, and re-layouts, local(): outgoing = gridded[:, send_slots]  22.6 us
    all_to_all x1, blocking collectives, local(): lax.all_to_all(columns, 'bin', split_axis=0, concat_axis=1, tiled=True)  21.2 us
  transfers between devices with their start and end apart: 3, of which 2 were waited for; matrix products, arithmetic and copies ran while one was open for 11% of the time, Pallas kernels for 0%

commit v1 on v0

v1 whole, which is shorter than its diff:
```python
import jax
import jax.numpy as jnp
from jax import lax
from jax.experimental import pallas as pl
from jax.experimental.pallas import tpu as pltpu
from jax.sharding import PartitionSpec as P

SUBSTEPS = 2
SRC = 5
SOURCE_DT = 0.25
TINY = 1e-06
GX = 256
GY = 32
BINS = 9
K = 1152
ROWS = 64
NB = 2048
SLOTS = 32
SOURCES = 128
STAGES = 13
f32, bf16, i32 = jnp.float32, jnp.bfloat16, jnp.int32


def iota(shape, dim):
    return lax.broadcasted_iota(i32, shape, dim)


def lanes(x, index):
    return jnp.take_along_axis(x, index, axis=1, mode="promise_in_bounds")


def pick(table, index):
    low = jnp.concatenate([table[:GY], table[:GY]], 0)
    high = jnp.concatenate([table[GY:], table[GY:]], 0)
    within = index & 127
    return jnp.where(index < 128, lanes(low, within), lanes(high, within))


def load_split(ref, *lead):
    return jnp.concatenate(
        [ref[(*lead, pl.ds(half, GY, stride=2), slice(None))] for half in range(2)], 0
    )


def linear_shift(x, amount):
    if amount >= 128:
        return pltpu.roll(x, ROWS - amount // 128, 0)
    turned = pltpu.roll(x, 128 - amount, 1)
    return jnp.where(iota(x.shape, 1) >= 128 - amount, pltpu.roll(turned, ROWS - 1, 0), turned)


def linear_unshift(x, amount):
    if amount >= 128:
        return pltpu.roll(x, amount // 128, 0)
    turned = pltpu.roll(x, amount, 1)
    return jnp.where(iota(x.shape, 1) < amount, pltpu.roll(turned, 1, 0), turned)


def col_shift(x, amount):
    lane = iota((GY, 128), 1)
    low = pltpu.roll(x[:GY], (128 - amount) % 128, 1)
    high = pltpu.roll(x[GY:], (128 - amount) % 128, 1)
    crossed = lane >= 128 - amount if amount > 0 else lane < -amount
    return jnp.concatenate([jnp.where(crossed, high, low), jnp.where(crossed, low, high)], 0)


def row_shift(x, amount):
    turn = (GY - amount) % GY
    return jnp.concatenate([pltpu.roll(x[:GY], turn, 0), pltpu.roll(x[GY:], turn, 0)], 0)


def advect(field, rate, shift):
    magnitude = jnp.abs(rate)
    forward = rate >= 0.0
    ahead = shift(field, 1)
    upwind = jnp.where(forward, field, ahead)
    downwind = jnp.where(forward, ahead, field)
    far_upwind = jnp.where(forward, shift(field, -1), shift(field, 2))
    estimate = (
        0.5 * (upwind + downwind)
        - 0.5 * magnitude * (downwind - upwind)
        - ((1.0 - magnitude * magnitude) * (1.0 / 6.0)) * (downwind - 2.0 * upwind + far_upwind)
    )
    low, high = jnp.minimum(upwind, downwind), jnp.maximum(upwind, downwind)
    face = jnp.minimum(jnp.maximum(estimate, low), high)
    return field - rate * (face - shift(face, -1))


def two_parts(x):
    high = x.astype(bf16)
    return high, (x - high.astype(f32)).astype(bf16)


def stage_rows(b, x, lhs):
    row = jnp.concatenate([x[:GY], x[GY:]], 1)
    high, rest = two_parts(row)
    lhs[b * GY : (b + 1) * GY, :] = high
    lhs[(BINS + b) * GY : (BINS + b + 1) * GY, :] = rest


def gather_send(send, lhs, out):
    def chunk(c, carry):
        at = pl.ds(pl.multiple_of(c * 256, 256), 256)
        point = send[:, at]
        onehot = (iota((GX, 256), 0) == (point & (GX - 1))).astype(f32).astype(bf16)
        found = jnp.dot(lhs[...], onehot, preferred_element_type=f32)
        mine = iota((GY, 256), 0) == (point // GX)
        rows = []
        for b in range(BINS):
            whole = found[b * GY : (b + 1) * GY] + found[(BINS + b) * GY : (BINS + b + 1) * GY]
            rows.append(jnp.sum(jnp.where(mine, whole, 0.0), axis=0, keepdims=True))
        out[:, at] = jnp.concatenate(rows, 0)
        return carry

    lax.fori_loop(0, NB // 256, chunk, 0, unroll=2)


def start_kernel(
    spectra, tables, wet, wind, send, field, index, sea_out, turn_out, words, wind_out, out, lhs
):
    def table(t, half):
        return tables[pl.ds(t + 4 * half, GY, stride=8), :]

    column = iota((ROWS, 128), 1) + jnp.where(iota((ROWS, 128), 0) >= GY, 128, 0)
    east = jnp.concatenate([table(0, 0), table(0, 1)], 0) & (GX - 1)
    west = jnp.concatenate([table(1, 0), table(1, 1)], 0) & (GX - 1)
    walk = jnp.where(column == 0, 0, west + GX)
    for _ in range(8):
        walk = (walk & -GX) + pick(walk, walk & (GX - 1))
    steps = walk >> 8
    reach, ring = jnp.zeros((ROWS, 128), i32), east
    for k in range(8):
        reach = jnp.where(((column >> k) & 1) == 1, pick(ring, reach), reach)
        if k < 7:
            ring = pick(ring, ring)

    north, south = table(2, 0), table(3, 0)
    upward = jnp.broadcast_to(north[0:1, 0:1], (GY, 128)) // GX == 1
    above = jnp.where(
        upward,
        jnp.broadcast_to(north[:, 0:1], (GY, 128)),
        jnp.broadcast_to(south[:, 0:1], (GY, 128)),
    ) & (GX - 1)
    above = pltpu.roll(above, 1, 0)
    within = above & 127
    offset = jnp.where(above < 128, lanes(steps[:GY], within), lanes(steps[GY:], within))
    offset = jnp.where(iota((GY, 128), 0) == 0, 0, offset)
    ladder = (iota((GY, GY), 1) <= iota((GY, GY), 0)).astype(f32).astype(bf16)
    total = jnp.dot(ladder, offset.astype(f32).astype(bf16), preferred_element_type=f32)
    start = (GX * GY - total.astype(i32)) & (GX - 1)
    start = jnp.concatenate([start, start], 0)
    index[0] = pick(reach, (column - start) & (GX - 1))
    index[1] = (steps + start) & (GX - 1)
    turn_out[...] = jnp.where(upward[:8], 1.0, -1.0)

    wet_int = load_split(wet)
    sea = wet_int.astype(f32)
    sea_out[...] = sea
    for b in range(BINS):
        x = load_split(spectra, b) * sea
        field[b] = x
        stage_rows(b, x, lhs)
    gather_send(send, lhs, out)

    dry = (1.0 - sea).astype(bf16)
    before = (iota((128, 128), 0) < iota((128, 128), 1)).astype(f32).astype(bf16)
    rows = jnp.dot(dry, jnp.ones((128, 128), bf16), preferred_element_type=f32)
    above_rows = (iota((ROWS, ROWS), 1) < iota((ROWS, ROWS), 0)).astype(f32).astype(bf16)
    move = jnp.dot(dry, before, preferred_element_type=f32) + jnp.dot(
        above_rows, rows.astype(bf16), preferred_element_type=f32
    )
    move = jnp.where(wet_int == 1, move.astype(i32), 0)
    windy = load_split(wind)
    leave, enter = jnp.zeros((ROWS, 128), i32), jnp.zeros((ROWS, 128), i32)
    for k in range(STAGES):
        going = (move >> k) & 1
        leave = leave | (going << k)
        other = linear_shift(move, 1 << k)
        coming = (other >> k) & 1
        enter = enter | (coming << k)
        move = jnp.where(coming == 1, other, jnp.where(going == 1, 0, move))
        windy = jnp.where(coming == 1, linear_shift(windy, 1 << k), windy)
    words[0] = leave
    words[1] = enter
    wind_out[...] = windy[:SLOTS]


def receive(incoming, recv, lhs, rhs):
    point = recv[...]
    rhs[...] = (iota((GX, NB), 0) == (point & (GX - 1))).astype(f32).astype(bf16)
    mine = iota((GY, NB), 0) == point // GX
    for b in range(BINS):
        value = incoming[b : b + 1, :]
        high = value.astype(bf16).astype(f32)
        lhs[b * GY : (b + 1) * GY, :] = jnp.where(mine, high, 0.0).astype(bf16)
        lhs[(BINS + b) * GY : (BINS + b + 1) * GY, :] = jnp.where(mine, value - high, 0.0).astype(bf16)
    lhs[2 * BINS * GY :, :] = jnp.where(mine, 1.0, 0.0).astype(bf16)
    return lax.dot_general(
        lhs[...], rhs[...], (((1,), (1,)), ((), ())), preferred_element_type=f32
    )


def substep(number, b, placed, field, courant, count, order, position, sea, turn):
    got = placed[b * GY : (b + 1) * GY] + placed[(BINS + b) * GY : (BINS + b + 1) * GY]
    hit = placed[2 * BINS * GY :]
    got = jnp.concatenate([got[:, :128], got[:, 128:]], 0)
    hit = jnp.concatenate([hit[:, :128], hit[:, 128:]], 0)
    old = field[b]
    x = jnp.where(hit > 0.5, got, old)
    scale = jnp.where(count[0] == 2, 0.5, 1.0)
    x = pick(x, order)
    x = advect(x, jnp.full((ROWS, 128), courant[0, b] * scale), col_shift)
    x = advect(x, (courant[1, b] * scale) * turn, row_shift)
    x = pick(x, position) * sea
    return x if number == 0 else jnp.where(number < count[0], x, old)


def first_kernel(
    incoming, recv, send, field, index, sea, turn, courant, count, field_out, out, lhs, wide, rhs
):
    placed = receive(incoming, recv, wide, rhs)
    turned = jnp.concatenate([turn[...]] * (ROWS // 8), 0)
    for b in range(BINS):
        x = substep(0, b, placed, field, courant, count, index[0], index[1], sea[...], turned)
        field_out[b] = x
        stage_rows(b, x, lhs)
    gather_send(send, lhs, out)


def last_kernel(
    incoming, recv, field, index, sea, turn, words, courant, count, packed, wide, rhs
):
    placed = receive(incoming, recv, wide, rhs)
    turned = jnp.concatenate([turn[...]] * (ROWS // 8), 0)
    enter = words[1]
    for b in range(BINS):
        x = substep(1, b, placed, field, courant, count, index[0], index[1], sea[...], turned)
        for k in range(STAGES):
            x = jnp.where(((enter >> k) & 1) == 1, linear_shift(x, 1 << k), x)
        packed[pl.ds(b, SLOTS, stride=BINS), :] = x[:SLOTS]


def device_of(slot, nest):
    return slot * 4 + lax.rem(2 * nest + 32 - slot // 8 - lax.rem(slot, 8), 4)


def source_kernel(
    packed, coupling, growth, dissipation, wind, back, columns, coarse, grown, damped,
    own_sem, send_sem, recv_sem, back_send, back_recv,
):
    nest, me = lax.axis_index("nest"), lax.axis_index("bin")
    slot = me // 4
    integrates = device_of(slot, nest) == me
    mine = jnp.where(integrates, 1, 0)

    def to(device):
        return {"bin": device}

    def forward(q):
        return pltpu.make_async_remote_copy(
            src_ref=packed.at[pl.ds(q * BINS, BINS)],
            dst_ref=columns.at[pl.ds(me * BINS, BINS)],
            send_sem=send_sem.at[q],
            recv_sem=recv_sem.at[me],
            device_id=to(device_of(q, nest)),
            device_id_type=pl.DeviceIdType.MESH,
        )

    def arriving(s):
        return pltpu.make_async_remote_copy(
            src_ref=packed.at[pl.ds(0, BINS)],
            dst_ref=columns.at[pl.ds(s * BINS, BINS)],
            send_sem=send_sem.at[0],
            recv_sem=recv_sem.at[s],
            device_id=to(s),
            device_id_type=pl.DeviceIdType.MESH,
        )

    def returning(s):
        return pltpu.make_async_remote_copy(
            src_ref=columns.at[pl.ds(s * BINS, BINS)],
            dst_ref=back.at[pl.ds(slot * BINS, BINS)],
            send_sem=back_send.at[s],
            recv_sem=back_recv.at[slot],
            device_id=to(s),
            device_id_type=pl.DeviceIdType.MESH,
        )

    def landing(q):
        return pltpu.make_async_remote_copy(
            src_ref=columns.at[pl.ds(0, BINS)],
            dst_ref=back.at[pl.ds(q * BINS, BINS)],
            send_sem=back_send.at[0],
            recv_sem=back_recv.at[q],
            device_id=to(device_of(q, nest)),
            device_id_type=pl.DeviceIdType.MESH,
        )

    def own_in():
        return pltpu.make_async_copy(
            packed.at[pl.ds(slot * BINS, BINS)], columns.at[pl.ds(me * BINS, BINS)], own_sem
        )

    def own_out():
        return pltpu.make_async_copy(
            columns.at[pl.ds(me * BINS, BINS)], back.at[pl.ds(slot * BINS, BINS)], own_sem
        )

    def each(count, first, skip, body):
        def step(i, carry):
            at = lax.rem(first + i, count)

            @pl.when(at != skip)
            def _():
                body(at)

            return carry

        lax.fori_loop(0, count, step, 0)

    skipped_slot = jnp.where(integrates, slot, -1)
    barrier = pltpu.get_barrier_semaphore()

    @pl.when(integrates)
    def _():
        def greet(s):
            pl.semaphore_signal(
                barrier, inc=1, device_id=to(s), device_id_type=pl.DeviceIdType.MESH
            )

        each(SOURCES, me, me, greet)

    for block in range(BINS):
        at = slice(block * 128, (block + 1) * 128)
        grown[at, :] = jnp.transpose(jnp.broadcast_to(SOURCE_DT * growth[:, at], (128, 128)))
        damped[at, :] = jnp.transpose(jnp.broadcast_to(SOURCE_DT * dissipation[:, at], (128, 128)))

    pl.semaphore_wait(barrier, SLOTS - mine)
    each(SLOTS, slot, skipped_slot, lambda q: forward(q).start())

    @pl.when(integrates)
    def _():
        own_in().start()
        each(SOURCES, me, me, lambda s: arriving(s).wait_recv())
        own_in().wait()
        windy = wind[pl.ds(slot, 1), :]

        def step(i, carry):
            v = columns[...]
            coarse[...] = v.astype(bf16)
            linear = jnp.dot(coupling[...], coarse[...], preferred_element_type=f32)
            rms = jnp.sqrt(jnp.sum(v * v, axis=0, keepdims=True) * (1.0 / K) + TINY)
            columns[...] = (v + (SOURCE_DT * linear + grown[...] * windy * v)) / (
                1.0 + damped[...] * rms
            )
            return carry

        lax.fori_loop(0, SRC, step, 0)
        each(SOURCES, me, me, lambda s: returning(s).start())
        own_out().start()
        own_out().wait()

    each(SLOTS, slot, skipped_slot, lambda q: landing(q).wait_recv())
    each(SLOTS, slot, skipped_slot, lambda q: forward(q).wait_send())

    @pl.when(integrates)
    def _():
        each(SOURCES, me, me, lambda s: returning(s).wait_send())


def finish_kernel(back, words, sea, result):
    leave = words[0]
    wet = sea[...] > 0.5
    for b in range(BINS):
        x = back[pl.ds(b, SLOTS, stride=BINS), :]
        x = jnp.concatenate([x, x], 0)
        for k in reversed(range(STAGES - 1)):
            x = jnp.where(((leave >> k) & 1) == 1, linear_unshift(x, 1 << k), x)
        x = jnp.where(wet, x, 0.0)
        for half in range(2):
            result[b, pl.ds(half, GY, stride=2), :] = x[half * GY : (half + 1) * GY]


def call(kernel, inputs, outputs, scratch=(), scalars=(), **params):
    vmem = pl.BlockSpec(memory_space=pltpu.VMEM)
    smem = pl.BlockSpec(memory_space=pltpu.SMEM)
    return pl.pallas_call(
        kernel,
        out_shape=[jax.ShapeDtypeStruct(*out) for out in outputs],
        in_specs=[vmem] * len(inputs) + [smem] * len(scalars),
        out_specs=[vmem] * len(outputs),
        scratch_shapes=list(scratch),
        compiler_params=pltpu.CompilerParams(**params),
    )(*inputs, *scalars)


def local(
    spectra, courant, coupling, growth, dissipation, wind,
    neighbours, wet_mask, send_list, recv_list, substep_count,
):
    def swap(array):
        return lax.ppermute(array, "nest", [(0, 1), (1, 0)])

    grid = ((BINS, ROWS, 128), f32)
    plane = (ROWS, 128)
    listed = ((BINS, NB), f32)
    lhs = pltpu.VMEM((2 * BINS * GY, GX), bf16)
    wide = pltpu.VMEM((2 * BINS * GY + GY, NB), bf16)
    rhs = pltpu.VMEM((GX, NB), bf16)
    tables = neighbours.reshape(4, ROWS, 128).transpose(1, 0, 2).reshape(4 * ROWS, 128)
    field, index, sea, turn, words, windy, out = call(
        start_kernel,
        [spectra.reshape(BINS, ROWS, 128), tables, wet_mask.reshape(plane), wind.reshape(plane), send_list],
        [grid, ((2, *plane), i32), (plane, f32), ((8, 128), f32), ((2, *plane), i32), ((SLOTS, 128), f32), listed],
        [lhs],
    )
    field, out = call(
        first_kernel,
        [swap(out), recv_list, send_list, field, index, sea, turn],
        [grid, listed],
        [lhs, wide, rhs],
        [courant, substep_count],
    )
    (packed,) = call(
        last_kernel,
        [swap(out), recv_list, field, index, sea, turn, words],
        [((SLOTS * BINS, 128), f32)],
        [wide, rhs],
        [courant, substep_count],
    )
    (back,) = call(
        source_kernel,
        [packed, coupling, growth.reshape(1, K), dissipation.reshape(1, K), windy],
        [((SLOTS * BINS, 128), f32)],
        [
            pltpu.VMEM((K, 128), f32), pltpu.VMEM((K, 128), bf16),
            pltpu.VMEM((K, 128), f32), pltpu.VMEM((K, 128), f32),
            pltpu.SemaphoreType.DMA,
            pltpu.SemaphoreType.DMA((SLOTS,)), pltpu.SemaphoreType.DMA((SOURCES,)),
            pltpu.SemaphoreType.DMA((SOURCES,)), pltpu.SemaphoreType.DMA((SLOTS,)),
        ],
        collective_id=0,
        has_side_effects=True,
    )
    (result,) = call(finish_kernel, [back, words, sea], [grid])
    return result.reshape(1, BINS, ROWS * 128)


def solution(mesh):
    in_specs = (
        P("nest", "bin", None), P(None, "bin"), P(), P(), P(), P("nest", None),
        P("nest", None, None), P("nest", None), P("nest", None), P("nest", None), P("nest"),
    )
    return jax.shard_map(
        local, mesh=mesh, in_specs=in_specs, out_specs=P("nest", "bin", None), check_vma=False
    )
```

time: 586 us -> 65.3 us (0.11)
  local copies, waits for them, and re-layouts: 477 us -> 3.88 us
  Pallas kernels: 0 us -> 58.6 us
  loops' own time: 24.8 us -> 0 us
  other arithmetic: 21.4 us -> 0 us
  blocking collectives: 21.2 us -> 0 us
  starting transfers between devices: 16.2 us -> 0.15 us
  waiting for transfers between devices: 15.7 us -> 0.91 us
  matrix products: 6.86 us -> 0 us
    gather x266 -> x0, local copies, waits for them, and re-layouts: 335 us -> none  [the longest x256 179 us: east_walk(): return (east_index[point], point)]
    pallas_call x0 -> x5, Pallas kernels: none -> 58.6 us  [call(): pl.pallas_call(kernel, out_shape=[jax.ShapeDtypeStruct(*out) for out in o...]
    scatter x5 -> x0, local copies, waits for them, and re-layouts: 57.7 us -> none  [the longest x1 30.5 us: local(): jnp.zeros((points,), jnp.int32).at[ordering]]
    another operation x2 -> x0, loops' own time: 24.8 us -> none  [the longest x1 20.6 us: grid_order(): starts = lax.scan(north_walk, jnp.int32(0), None, length=rows_count)[1]]
    all_to_all x1 -> x0, blocking collectives: 21.2 us -> none  [local(): lax.all_to_all(columns, 'bin', split_axis=0, concat_axis=1, tiled=True)]
    dynamic_slice x32 -> x0, local copies, waits for them, and re-layouts: 20.8 us -> none  [north_walk(): return (north_index[point], point)]
    all_to_all x1 -> x0, starting transfers between devices: 15.6 us -> none  [local(): lax.all_to_all(field, 'bin', split_axis=1, concat_axis=0, tiled=True)]
    unnamed x78 -> x4, local copies, waits for them, and re-layouts: 16.8 us -> 1.3 us
  transfers between devices with their start and end apart: 3 -> 2, of which waited for: 2 -> 1; matrix products, arithmetic and copies ran while one was open for 11% -> 4% of each run, Pallas kernels for 0% -> 0%
where the time goes in v1:
time: 65.3 us; the launch traced here: 64.2 us
  Pallas kernels  58.6 us (90%)
  local copies, waits for them, and re-layouts  3.88 us (6%)
  waiting for transfers between devices  0.91 us (1%)
  between operations  0.67 us (1%)
    pallas_call x5, Pallas kernels, call(): pl.pallas_call(kernel, out_shape=[jax.ShapeDtypeStruct(*out) for out in o...  58.6 us
  transfers between devices with their start and end apart: 2, of which 1 were waited for; matrix products, arithmetic and copies ran while one was open for 4% of the time, Pallas kernels for 0%

profile of v1, /device:TPU:2, one launch (start us, length us, event | category | flops | bytes accessed | tf_op | source)
XLA Modules:
  0.0 64.2 jit_solution(2676393343738773796)
XLA Ops:
  0.0 5.6 %shard_map.109 = (f32[9,64,128]{2,1,0:T(8,128)}, s32[2,64,128]{2,1,0:T(8,128)}, f32[64,128]{1,0:T(8,128)}, f32[8,128]{1,0:T(8,128)}, s32[2,64,128]{2,1,0:T(8,128...) custom-call(f32[9,64,128]{2,1,0:T(8,128)} %bitcast.9, s32[256,128]{1,0:T(8,128)} %bitcast.10, s32[64,128]{1,0:T(8,128)} %bitcast.11, ...), custom_call_target="tpu_custom_call" | custom-call | tf_op jit(solution)/shard_map/pallas_call | solution.py:387
  5.6 0.0 collective-permute-start
  6.2 0.9 %collective-permute-done.incoming = f32[9,2048]{1,0:T(8,128)S(1)} collective-permute-done((f32[9,2048]{1,0:T(8,128)}, f32[9,2048]{1,0:T(8,128)S(1)}, u32[]{:S(2)}, u32[]{:S(2)}) %collective-permute-start) | collective-permute-done | bytes 73760 | tf_op jit(solution)/shard_map/ppermute | solution.py:402
  7.1 0.0 copy-start.1
  7.1 0.6 %copy-done.1 = f32[9,2048]{1,0:T(8,128)} copy-done((f32[9,2048]{1,0:T(8,128)}, f32[9,2048]{1,0:T(8,128)S(1)}, u32[]{:S(2)}) %copy-start.1) | copy-done | bytes 73752
  7.8 5.2 %shard_map.110 = (f32[9,64,128]{2,1,0:T(8,128)}, f32[9,2048]{1,0:T(8,128)}) custom-call(f32[9,2048]{1,0:T(8,128)} %copy-done.1, s32[1,2048]{1,0:T(1,128)} %recv.3, s32[1,2048]{1,0:T(1,128)} %send.3, f32[9,64,128]{2,1,0:T(8,128)} %get-tuple-element.15.field, s32[2,64,128]{2,1,0:T(8,128)} %get-tuple-element.16.index, f32[64,128]{1,0:T(8,128)} %get-tuple-element.17.sea, ...), custom_call_target="tpu_custom_call" | custom-call | tf_op jit(solution)/shard_map/pallas_call | solution.py:387
  13.0 0.1 collective-permute-start.1
  13.1 1.3 %reshape.29.growth = f32[1,1152]{1,0:T(1,128)} reshape(f32[1152]{0:T(1024)} %param.14) | data formatting | bytes 9216 | tf_op jit(solution)/shard_map/reshape | solution.py:433
  14.4 1.3 %reshape.30.dissipation = f32[1,1152]{1,0:T(1,128)} reshape(f32[1152]{0:T(1024)} %param.15) | data formatting | bytes 9216 | tf_op jit(solution)/shard_map/reshape | solution.py:433
  15.7 0.0 collective-permute-done.1.incoming
  15.7 0.0 copy-start
  15.7 0.6 %copy-done = f32[9,2048]{1,0:T(8,128)} copy-done((f32[9,2048]{1,0:T(8,128)}, f32[9,2048]{1,0:T(8,128)S(1)}, u32[]{:S(2)}) %copy-start) | copy-done | bytes 73752
  16.4 4.6 %shard_map.111.packed = f32[288,128]{1,0:T(8,128)} custom-call(f32[9,2048]{1,0:T(8,128)} %copy-done, s32[1,2048]{1,0:T(1,128)} %recv.3, f32[9,64,128]{2,1,0:T(8,128)} %get-tuple-element.20.field, s32[2,64,128]{2,1,0:T(8,128)} %get-tuple-element.16.index, f32[64,128]{1,0:T(8,128)} %get-tuple-element.17.sea, f32[8,128]{1,0:T(8,128)} %get-tuple-element.18.turn, ...), custom_call_target="tpu_custom_call" | custom-call | tf_op jit(solution)/shard_map/pallas_call | solution.py:387
  21.0 40.7 %shard_map.112.back = f32[288,128]{1,0:T(8,128)} custom-call(f32[288,128]{1,0:T(8,128)} %shard_map.111.packed, bf16[1152,1152]{1,0:T(8,128)(2,1)} %coupling.1, f32[1,1152]{1,0:T(1,128)} %reshape.29.growth, f32[1,1152]{1,0:T(1,128)} %reshape.30.dissipation, f32[32,128]{1,0:T(8,128)} %get-tuple-element.22.wind), custom_call_target="tpu_custom_call" | custom-call | tf_op jit(solution)/shard_map/pallas_call | solution.py:387
  61.7 2.5 %shard_map.113 = f32[9,64,128]{2,1,0:T(8,128)} custom-call(f32[288,128]{1,0:T(8,128)} %shard_map.112.back, s32[2,64,128]{2,1,0:T(8,128)} %get-tuple-element.21.words, f32[64,128]{1,0:T(8,128)} %get-tuple-element.17.sea), custom_call_target="tpu_custom_call" | custom-call | tf_op jit(solution)/shard_map/pallas_call | solution.py:387
Async XLA Ops:
  5.6 1.6 %collective-permute-start = (f32[9,2048]{1,0:T(8,128)}, f32[9,2048]{1,0:T(8,128)S(1)}, u32[]{:S(2)}, u32[]{:S(2)}) collective-permute-start(f32[9,2048]{1,0:T(8,128)} %get-tuple-element.14), channel_id=1, source_target_pairs={{0,128},{128,0},{1,129},{129,1},{2,130},{130,2},{3,131},{131,3},{4... | collective-permute-start | bytes 221192 | tf_op jit(solution)/shard_map/ppermute | solution.py:402
  7.1 0.7 %copy-start.1 = (f32[9,2048]{1,0:T(8,128)}, f32[9,2048]{1,0:T(8,128)S(1)}, u32[]{:S(2)}) copy-start(f32[9,2048]{1,0:T(8,128)S(1)} %collective-permute-done.incoming) | copy-start | bytes 221188
  13.0 2.7 %collective-permute-start.1 = (f32[9,2048]{1,0:T(8,128)}, f32[9,2048]{1,0:T(8,128)S(1)}, u32[]{:S(2)}, u32[]{:S(2)}) collective-permute-start(f32[9,2048]{1,0:T(8,128)} %get-tuple-element.19), channel_id=1, source_target_pairs={{0,128},{128,0},{1,129},{129,1},{2,130},{130,2},{3,131},{131,3},{4... | collective-permute-start | bytes 221192 | tf_op jit(solution)/shard_map/ppermute | solution.py:402
  15.7 0.7 %copy-start = (f32[9,2048]{1,0:T(8,128)}, f32[9,2048]{1,0:T(8,128)S(1)}, u32[]{:S(2)}) copy-start(f32[9,2048]{1,0:T(8,128)S(1)} %collective-permute-done.1.incoming) | copy-start | bytes 221188

commit v2 on v1

v2 whole, which is shorter than its diff:
```python
import jax
import jax.numpy as jnp
from jax import lax
from jax.experimental import pallas as pl
from jax.experimental.pallas import tpu as pltpu
from jax.sharding import PartitionSpec as P

SUBSTEPS = 2
SRC = 5
SOURCE_DT = 0.25
TINY = 1e-06
GX = 256
GY = 32
BINS = 9
K = 1152
ROWS = 64
NB = 2048
SLOTS = 32
SOURCES = 128
STAGES = 13
f32, bf16, i32 = jnp.float32, jnp.bfloat16, jnp.int32


def iota(shape, dim):
    return lax.broadcasted_iota(i32, shape, dim)


def lanes(x, index):
    return jnp.take_along_axis(x, index, axis=1, mode="promise_in_bounds")


def pick(table, index):
    low = jnp.concatenate([table[:GY], table[:GY]], 0)
    high = jnp.concatenate([table[GY:], table[GY:]], 0)
    within = index & 127
    return jnp.where(index < 128, lanes(low, within), lanes(high, within))


def load_split(ref, *lead):
    return jnp.concatenate(
        [ref[(*lead, pl.ds(half, GY, stride=2), slice(None))] for half in range(2)], 0
    )


def linear_shift(x, amount):
    if amount >= 128:
        return pltpu.roll(x, ROWS - amount // 128, 0)
    turned = pltpu.roll(x, 128 - amount, 1)
    return jnp.where(iota(x.shape, 1) >= 128 - amount, pltpu.roll(turned, ROWS - 1, 0), turned)


def linear_unshift(x, amount):
    if amount >= 128:
        return pltpu.roll(x, amount // 128, 0)
    turned = pltpu.roll(x, amount, 1)
    return jnp.where(iota(x.shape, 1) < amount, pltpu.roll(turned, 1, 0), turned)


def col_shift(x, amount):
    lane = iota((GY, 128), 1)
    low = pltpu.roll(x[:GY], (128 - amount) % 128, 1)
    high = pltpu.roll(x[GY:], (128 - amount) % 128, 1)
    crossed = lane >= 128 - amount if amount > 0 else lane < -amount
    return jnp.concatenate([jnp.where(crossed, high, low), jnp.where(crossed, low, high)], 0)


def row_shift(x, amount):
    turn = (GY - amount) % GY
    return jnp.concatenate([pltpu.roll(x[:GY], turn, 0), pltpu.roll(x[GY:], turn, 0)], 0)


def advect(field, rate, shift):
    magnitude = jnp.abs(rate)
    forward = rate >= 0.0
    ahead = shift(field, 1)
    upwind = jnp.where(forward, field, ahead)
    downwind = jnp.where(forward, ahead, field)
    far_upwind = jnp.where(forward, shift(field, -1), shift(field, 2))
    estimate = (
        0.5 * (upwind + downwind)
        - 0.5 * magnitude * (downwind - upwind)
        - ((1.0 - magnitude * magnitude) * (1.0 / 6.0)) * (downwind - 2.0 * upwind + far_upwind)
    )
    low, high = jnp.minimum(upwind, downwind), jnp.maximum(upwind, downwind)
    face = jnp.minimum(jnp.maximum(estimate, low), high)
    return field - rate * (face - shift(face, -1))


def two_parts(x):
    high = x.astype(bf16)
    return high, (x - high.astype(f32)).astype(bf16)


def stage_rows(b, x, lhs):
    row = jnp.concatenate([x[:GY], x[GY:]], 1)
    high, rest = two_parts(row)
    lhs[b * GY : (b + 1) * GY, :] = high
    lhs[(BINS + b) * GY : (BINS + b + 1) * GY, :] = rest


def gather_send(send, chosen, lhs, out):
    def chunk(c, carry):
        at = pl.ds(pl.multiple_of(c * 256, 256), 256)
        point = send[:, at]
        found = jnp.dot(lhs[...], chosen[:, at], preferred_element_type=f32)
        mine = iota((GY, 256), 0) == (point // GX)
        rows = []
        for b in range(BINS):
            whole = found[b * GY : (b + 1) * GY] + found[(BINS + b) * GY : (BINS + b + 1) * GY]
            rows.append(jnp.sum(jnp.where(mine, whole, 0.0), axis=0, keepdims=True))
        out[:, at] = jnp.concatenate(rows, 0)
        return carry

    lax.fori_loop(0, NB // 256, chunk, 0, unroll=2)


def grid_order(tables):
    def table(t, half):
        return tables[pl.ds(t + 4 * half, GY, stride=8), :]

    column = iota((ROWS, 128), 1) + jnp.where(iota((ROWS, 128), 0) >= GY, 128, 0)
    east = jnp.concatenate([table(0, 0), table(0, 1)], 0) & (GX - 1)
    west = jnp.concatenate([table(1, 0), table(1, 1)], 0) & (GX - 1)
    walk = jnp.where(column == 0, 0, west + GX)
    for _ in range(8):
        walk = (walk & -GX) + pick(walk, walk & (GX - 1))
    steps = walk >> 8
    reach, ring = jnp.zeros((ROWS, 128), i32), east
    for k in range(8):
        reach = jnp.where(((column >> k) & 1) == 1, pick(ring, reach), reach)
        if k < 7:
            ring = pick(ring, ring)

    north, south = table(2, 0), table(3, 0)
    upward = jnp.broadcast_to(north[0:1, 0:1], (GY, 128)) // GX == 1
    above = jnp.where(
        upward,
        jnp.broadcast_to(north[:, 0:1], (GY, 128)),
        jnp.broadcast_to(south[:, 0:1], (GY, 128)),
    ) & (GX - 1)
    above = pltpu.roll(above, 1, 0)
    within = above & 127
    offset = jnp.where(above < 128, lanes(steps[:GY], within), lanes(steps[GY:], within))
    offset = jnp.where(iota((GY, 128), 0) == 0, 0, offset)
    ladder = (iota((GY, GY), 1) <= iota((GY, GY), 0)).astype(f32).astype(bf16)
    total = jnp.dot(ladder, offset.astype(f32).astype(bf16), preferred_element_type=f32)
    start = (GX * GY - total.astype(i32)) & (GX - 1)
    start = jnp.concatenate([start, start], 0)
    order = pick(reach, (column - start) & (GX - 1))
    return order, (steps + start) & (GX - 1), jnp.where(upward[:8], 1.0, -1.0)


def packing(wet_int, windy):
    dry = (1.0 - wet_int.astype(f32)).astype(bf16)
    before = (iota((128, 128), 0) < iota((128, 128), 1)).astype(f32).astype(bf16)
    rows = jnp.dot(dry, jnp.ones((128, 128), bf16), preferred_element_type=f32)
    above_rows = (iota((ROWS, ROWS), 1) < iota((ROWS, ROWS), 0)).astype(f32).astype(bf16)
    move = jnp.dot(dry, before, preferred_element_type=f32) + jnp.dot(
        above_rows, rows.astype(bf16), preferred_element_type=f32
    )
    move = jnp.where(wet_int == 1, move.astype(i32), 0)
    leave, enter = jnp.zeros((ROWS, 128), i32), jnp.zeros((ROWS, 128), i32)
    for k in range(STAGES):
        going = (move >> k) & 1
        leave = leave | (going << k)
        other = linear_shift(move, 1 << k)
        coming = (other >> k) & 1
        enter = enter | (coming << k)
        move = jnp.where(coming == 1, other, jnp.where(going == 1, 0, move))
        windy = jnp.where(coming == 1, linear_shift(windy, 1 << k), windy)
    return leave, enter, windy[:SLOTS]


def receive(incoming, recv, lhs, rhs):
    mine = iota((GY, NB), 0) == recv[...] // GX
    for b in range(BINS):
        value = incoming[b : b + 1, :]
        high = value.astype(bf16).astype(f32)
        lhs[b * GY : (b + 1) * GY, :] = jnp.where(mine, high, 0.0).astype(bf16)
        lhs[(BINS + b) * GY : (BINS + b + 1) * GY, :] = jnp.where(mine, value - high, 0.0).astype(bf16)
    lhs[2 * BINS * GY :, :] = jnp.where(mine, 1.0, 0.0).astype(bf16)
    return lax.dot_general(
        lhs[...], rhs[...], (((1,), (1,)), ((), ())), preferred_element_type=f32
    )


def substep(number, b, placed, field, courant, count, order, position, sea, turn):
    got = placed[b * GY : (b + 1) * GY] + placed[(BINS + b) * GY : (BINS + b + 1) * GY]
    hit = placed[2 * BINS * GY :]
    got = jnp.concatenate([got[:, :128], got[:, 128:]], 0)
    hit = jnp.concatenate([hit[:, :128], hit[:, 128:]], 0)
    old = field[b]
    x = jnp.where(hit > 0.5, got, old)
    scale = jnp.where(count[0] == 2, 0.5, 1.0)
    x = pick(x, order)
    x = advect(x, jnp.full((ROWS, 128), courant[0, b] * scale), col_shift)
    x = advect(x, (courant[1, b] * scale) * turn, row_shift)
    x = pick(x, position) * sea
    return x if number == 0 else jnp.where(number < count[0], x, old)


def device_of(slot, nest):
    return slot * 4 + lax.rem(2 * nest + 32 - slot // 8 - lax.rem(slot, 8), 4)


def step_kernel(
    spectra, tables, wet, wind, send, recv, growth, dissipation, coupling, courant, count, result,
    field, lhs, wide, chosen, placed_at, going, coming, packed, windy,
    columns, coarse, grown, damped, weights, back,
    weight_sem, swap_send, swap_recv, own_sem, send_sem, recv_sem, back_send, back_recv,
):
    nest, me = lax.axis_index("nest"), lax.axis_index("bin")
    slot = me // 4
    integrates = device_of(slot, nest) == me
    mine = jnp.where(integrates, 1, 0)

    def to(device):
        return {"bin": device}

    def forward(q):
        return pltpu.make_async_remote_copy(
            src_ref=packed.at[pl.ds(q * BINS, BINS)],
            dst_ref=columns.at[pl.ds(me * BINS, BINS)],
            send_sem=send_sem,
            recv_sem=recv_sem,
            device_id=to(device_of(q, nest)),
            device_id_type=pl.DeviceIdType.MESH,
        )

    def returning(s):
        return pltpu.make_async_remote_copy(
            src_ref=columns.at[pl.ds(s * BINS, BINS)],
            dst_ref=back.at[pl.ds(slot * BINS, BINS)],
            send_sem=back_send,
            recv_sem=back_recv,
            device_id=to(s),
            device_id_type=pl.DeviceIdType.MESH,
        )

    def several(count, ref, sent, received):
        rows = ref.at[pl.ds(0, count * BINS)]
        return pltpu.make_async_remote_copy(
            src_ref=rows,
            dst_ref=rows,
            send_sem=sent,
            recv_sem=received,
            device_id=to(lax.rem(me + 1, SOURCES)),
            device_id_type=pl.DeviceIdType.MESH,
        )

    def own_in():
        return pltpu.make_async_copy(
            packed.at[pl.ds(slot * BINS, BINS)], columns.at[pl.ds(me * BINS, BINS)], own_sem
        )

    def own_out():
        return pltpu.make_async_copy(
            columns.at[pl.ds(me * BINS, BINS)], back.at[pl.ds(slot * BINS, BINS)], own_sem
        )

    def others(count, own):
        return [lax.rem(own + i, count) for i in range(1, count)]

    def swap(number):
        return pltpu.make_async_remote_copy(
            src_ref=going.at[number],
            dst_ref=coming.at[number],
            send_sem=swap_send.at[number],
            recv_sem=swap_recv.at[number],
            device_id={"nest": 1 - nest},
            device_id_type=pl.DeviceIdType.MESH,
        )

    barrier = pltpu.get_barrier_semaphore()
    pl.semaphore_signal(
        barrier, inc=1, device_id={"nest": 1 - nest}, device_id_type=pl.DeviceIdType.MESH
    )

    @pl.when(integrates)
    def _():
        for s in others(SOURCES, me):
            pl.semaphore_signal(
                barrier, inc=1, device_id=to(s), device_id_type=pl.DeviceIdType.MESH
            )

    fetch = pltpu.make_async_copy(coupling, weights, weight_sem)
    fetch.start()

    wet_int = load_split(wet)
    sea = wet_int.astype(f32)
    for b in range(BINS):
        x = load_split(spectra, b) * sea
        field[b] = x
        stage_rows(b, x, lhs)
    chosen[...] = (iota((GX, NB), 0) == (send[...] & (GX - 1))).astype(f32).astype(bf16)
    placed_at[...] = (iota((GX, NB), 0) == (recv[...] & (GX - 1))).astype(f32).astype(bf16)
    gather_send(send, chosen, lhs, going.at[0])
    order, position, turn = grid_order(tables)
    turn = jnp.concatenate([turn] * (ROWS // 8), 0)

    pl.semaphore_wait(barrier, SLOTS - mine + 1)
    swap(0).start()
    leave, enter, windy[...] = packing(wet_int, load_split(wind))
    swap(0).wait_recv()

    placed = receive(coming.at[0], recv, wide, placed_at)
    for b in range(BINS):
        x = substep(0, b, placed, field, courant, count, order, position, sea, turn)
        field[b] = x
        stage_rows(b, x, lhs)
    gather_send(send, chosen, lhs, going.at[1])
    swap(1).start()
    for block in range(BINS):
        at = slice(block * 128, (block + 1) * 128)
        grown[at, :] = jnp.transpose(jnp.broadcast_to((SOURCE_DT * growth[at]).reshape(1, 128), (128, 128)))
        damped[at, :] = jnp.transpose(jnp.broadcast_to((SOURCE_DT * dissipation[at]).reshape(1, 128), (128, 128)))
    swap(1).wait_recv()

    placed = receive(coming.at[1], recv, wide, placed_at)
    for b in range(BINS):
        x = substep(1, b, placed, field, courant, count, order, position, sea, turn)
        for k in range(STAGES):
            x = jnp.where(((enter >> k) & 1) == 1, linear_shift(x, 1 << k), x)
        packed[pl.ds(b, SLOTS, stride=BINS), :] = x[:SLOTS]

    for q in others(SLOTS, slot):
        forward(q).start()
    fetch.wait()

    @pl.when(jnp.logical_not(integrates))
    def _():
        forward(slot).start()

    @pl.when(integrates)
    def _():
        own_in().start()
        several(SOURCES - 1, columns, send_sem, recv_sem).wait_recv()
        own_in().wait()
        blown = windy[pl.ds(slot, 1), :]

        def step(i, carry):
            v = columns[...]
            coarse[...] = v.astype(bf16)
            linear = jnp.dot(weights[...], coarse[...], preferred_element_type=f32)
            rms = jnp.sqrt(jnp.sum(v * v, axis=0, keepdims=True) * (1.0 / K) + TINY)
            columns[...] = (v + (SOURCE_DT * linear + grown[...] * blown * v)) / (
                1.0 + damped[...] * rms
            )
            return carry

        lax.fori_loop(0, SRC, step, 0)
        for s in others(SOURCES, me):
            returning(s).start()
        own_out().start()
        own_out().wait()
        several(SLOTS - 1, back, back_send, back_recv).wait_recv()

    @pl.when(jnp.logical_not(integrates))
    def _():
        several(SLOTS, back, back_send, back_recv).wait_recv()

    wet_here = sea > 0.5
    for b in range(BINS):
        x = back[pl.ds(b, SLOTS, stride=BINS), :]
        x = jnp.concatenate([x, x], 0)
        for k in reversed(range(STAGES - 1)):
            x = jnp.where(((leave >> k) & 1) == 1, linear_unshift(x, 1 << k), x)
        x = jnp.where(wet_here, x, 0.0)
        for half in range(2):
            result[b, pl.ds(half, GY, stride=2), :] = x[half * GY : (half + 1) * GY]

    for number in range(SUBSTEPS):
        swap(number).wait_send()

    @pl.when(integrates)
    def _():
        several(SLOTS - 1, packed, send_sem, recv_sem).wait_send()
        several(SOURCES - 1, columns, back_send, back_recv).wait_send()

    @pl.when(jnp.logical_not(integrates))
    def _():
        several(SLOTS, packed, send_sem, recv_sem).wait_send()


def local(
    spectra, courant, coupling, growth, dissipation, wind,
    neighbours, wet_mask, send_list, recv_list, substep_count,
):
    plane = (ROWS, 128)
    tables = neighbours.reshape(4, ROWS, 128).transpose(1, 0, 2).reshape(4 * ROWS, 128)
    vmem = pl.BlockSpec(memory_space=pltpu.VMEM)
    smem = pl.BlockSpec(memory_space=pltpu.SMEM)
    result = pl.pallas_call(
        step_kernel,
        out_shape=jax.ShapeDtypeStruct((BINS, ROWS, 128), f32),
        in_specs=[vmem] * 8 + [pl.BlockSpec(memory_space=pl.ANY), smem, smem],
        out_specs=vmem,
        scratch_shapes=[
            pltpu.VMEM((BINS, ROWS, 128), f32),
            pltpu.VMEM((2 * BINS * GY, GX), bf16),
            pltpu.VMEM((2 * BINS * GY + GY, NB), bf16),
            pltpu.VMEM((GX, NB), bf16),
            pltpu.VMEM((GX, NB), bf16),
            pltpu.VMEM((SUBSTEPS, BINS, NB), f32),
            pltpu.VMEM((SUBSTEPS, BINS, NB), f32),
            pltpu.VMEM((SLOTS * BINS, 128), f32),
            pltpu.VMEM((SLOTS, 128), f32),
            pltpu.VMEM((K, 128), f32),
            pltpu.VMEM((K, 128), bf16),
            pltpu.VMEM((K, 128), f32),
            pltpu.VMEM((K, 128), f32),
            pltpu.VMEM((K, K), bf16),
            pltpu.VMEM((SLOTS * BINS, 128), f32),
            pltpu.SemaphoreType.DMA,
            pltpu.SemaphoreType.DMA((SUBSTEPS,)),
            pltpu.SemaphoreType.DMA((SUBSTEPS,)),
            pltpu.SemaphoreType.DMA,
            pltpu.SemaphoreType.DMA,
            pltpu.SemaphoreType.DMA,
            pltpu.SemaphoreType.DMA,
            pltpu.SemaphoreType.DMA,
        ],
        compiler_params=pltpu.CompilerParams(collective_id=0, has_side_effects=True),
    )(
        spectra.reshape(BINS, ROWS, 128), tables, wet_mask.reshape(plane), wind.reshape(plane),
        send_list, recv_list, growth, dissipation, coupling,
        courant, substep_count,
    )
    return result.reshape(1, BINS, ROWS * 128)


def solution(mesh):
    in_specs = (
        P("nest", "bin", None), P(None, "bin"), P(), P(), P(), P("nest", None),
        P("nest", None, None), P("nest", None), P("nest", None), P("nest", None), P("nest"),
    )
    return jax.shard_map(
        local, mesh=mesh, in_specs=in_specs, out_specs=P("nest", "bin", None), check_vma=False
    )
```

time: 65.3 us -> 48.4 us (0.74)
  Pallas kernels: 58.6 us -> 45.5 us
  local copies, waits for them, and re-layouts: 3.88 us -> 1.69 us
  waiting for transfers between devices: 0.91 us -> 0 us
    pallas_call x5 -> x1, Pallas kernels: 58.6 us -> 45.5 us  [local(): pl.pallas_call(step_kernel, out_shape=jax.ShapeDtypeStruct((BINS, ROWS, 1...]
    reshape x2 -> x0, local copies, waits for them, and re-layouts: 2.58 us -> none  [the longest x1 1.29 us: local(): growth.reshape(1, K)]
    ppermute x2 -> x0, waiting for transfers between devices: 0.91 us -> none  [swap(): return lax.ppermute(array, 'nest', [(0, 1), (1, 0)])]
    unnamed x4 -> x1, local copies, waits for them, and re-layouts: 1.3 us -> 1.69 us
  transfers between devices with their start and end apart: 2 -> 0, of which waited for: 1 -> 0; matrix products, arithmetic and copies ran while one was open for 4% -> 0% of each run, Pallas kernels for 0% -> 0%
where the time goes in v2:
time: 48.4 us; the launch traced here: 47.8 us
  Pallas kernels  45.5 us (94%)
  local copies, waits for them, and re-layouts  1.69 us (3%)
  between operations  0.66 us (1%)
    pallas_call x1, Pallas kernels, local(): pl.pallas_call(step_kernel, out_shape=jax.ShapeDtypeStruct((BINS, ROWS, 1...  45.5 us
    unnamed x1, local copies, waits for them, and re-layouts  1.69 us

profile of v2, /device:TPU:2, one launch (start us, length us, event | category | flops | bytes accessed | tf_op | source)
XLA Modules:
  0.0 47.8 jit_solution(9676791521146618662)
XLA Ops:
  0.7 45.5 %shard_map.109 = f32[9,64,128]{2,1,0:T(8,128)} custom-call(f32[9,64,128]{2,1,0:T(8,128)} %bitcast.10, s32[256,128]{1,0:T(8,128)} %bitcast.11, s32[64,128]{1,0:T(8,128)} %bitcast.12, f32[64,128]{1,0:T(8,128)} %bitcast.13, s32[1,2048]{1,0:T(1,128)} %send.1, s32[1,2048]{1,0:T(1,128)} %recv.1, f32[1152]{0:T(1024)} %growth.1, f32[1152]{0:T(1024)} %dissipation.1, ...), custom_call_target="tpu_custom_call" | custom-call | tf_op jit(solution)/shard_map/pallas_call | solution.py:393
  46.1 1.7 %copy.18 = f32[1,9,8192]{2,0,1:T(1,128)} copy(f32[1,9,8192]{2,0,1:T(1,128)} %bitcast.9) | data formatting | bytes 589824

commit v3 on v2

--- a/solution.py
+++ b/solution.py
@@ -86,6 +86,11 @@
     return field - rate * (face - shift(face, -1))
 
 
+def onehot(within):
+    rows = iota((GX, NB), 0).astype(f32).astype(bf16)
+    return jnp.where(rows == within.astype(f32).astype(bf16), jnp.ones((), bf16), jnp.zeros((), bf16))
+
+
 def two_parts(x):
     high = x.astype(bf16)
     return high, (x - high.astype(f32)).astype(bf16)
@@ -99,19 +104,16 @@
 
 
 def gather_send(send, chosen, lhs, out):
-    def chunk(c, carry):
-        at = pl.ds(pl.multiple_of(c * 256, 256), 256)
+    for c in range(NB // 256):
+        at = slice(c * 256, (c + 1) * 256)
         point = send[:, at]
         found = jnp.dot(lhs[...], chosen[:, at], preferred_element_type=f32)
-        mine = iota((GY, 256), 0) == (point // GX)
+        mine = iota((GY, 256), 0) == (point >> 8)
         rows = []
         for b in range(BINS):
             whole = found[b * GY : (b + 1) * GY] + found[(BINS + b) * GY : (BINS + b + 1) * GY]
             rows.append(jnp.sum(jnp.where(mine, whole, 0.0), axis=0, keepdims=True))
         out[:, at] = jnp.concatenate(rows, 0)
-        return carry
-
-    lax.fori_loop(0, NB // 256, chunk, 0, unroll=2)
 
 
 def grid_order(tables):
@@ -172,58 +174,100 @@
 
 
 def receive(incoming, recv, lhs, rhs):
-    mine = iota((GY, NB), 0) == recv[...] // GX
+    row = (recv[...] >> 8).astype(f32).astype(bf16)
+    mine = iota((GY, NB), 0).astype(f32).astype(bf16) == row
+    zero = jnp.zeros((), bf16)
     for b in range(BINS):
-        value = incoming[b : b + 1, :]
-        high = value.astype(bf16).astype(f32)
-        lhs[b * GY : (b + 1) * GY, :] = jnp.where(mine, high, 0.0).astype(bf16)
-        lhs[(BINS + b) * GY : (BINS + b + 1) * GY, :] = jnp.where(mine, value - high, 0.0).astype(bf16)
-    lhs[2 * BINS * GY :, :] = jnp.where(mine, 1.0, 0.0).astype(bf16)
+        high, rest = two_parts(incoming[b : b + 1, :])
+        lhs[b * GY : (b + 1) * GY, :] = jnp.where(mine, jnp.broadcast_to(high, (GY, NB)), zero)
+        lhs[(BINS + b) * GY : (BINS + b + 1) * GY, :] = jnp.where(
+            mine, jnp.broadcast_to(rest, (GY, NB)), zero
+        )
+    lhs[2 * BINS * GY :, :] = jnp.where(mine, jnp.ones((), bf16), zero)
     return lax.dot_general(
         lhs[...], rhs[...], (((1,), (1,)), ((), ())), preferred_element_type=f32
     )
 
 
-def substep(number, b, placed, field, courant, count, order, position, sea, turn):
-    got = placed[b * GY : (b + 1) * GY] + placed[(BINS + b) * GY : (BINS + b + 1) * GY]
+def pick_each(tables, index):
+    parts = [[] for _ in tables]
+    for at in range(0, ROWS, 8):
+        low = at % GY
+        here = index[at : at + 8]
+        within, first = here & 127, here < 128
+        for part, table in zip(parts, tables):
+            part.append(
+                jnp.where(
+                    first,
+                    lanes(table[low : low + 8], within),
+                    lanes(table[GY + low : GY + low + 8], within),
+                )
+            )
+    return [jnp.concatenate(part, 0) for part in parts]
+
+
+def substep(number, placed, field, courant, count, order, position, sea, turn):
     hit = placed[2 * BINS * GY :]
-    got = jnp.concatenate([got[:, :128], got[:, 128:]], 0)
-    hit = jnp.concatenate([hit[:, :128], hit[:, 128:]], 0)
-    old = field[b]
-    x = jnp.where(hit > 0.5, got, old)
-    scale = jnp.where(count[0] == 2, 0.5, 1.0)
-    x = pick(x, order)
-    x = advect(x, jnp.full((ROWS, 128), courant[0, b] * scale), col_shift)
-    x = advect(x, (courant[1, b] * scale) * turn, row_shift)
-    x = pick(x, position) * sea
-    return x if number == 0 else jnp.where(number < count[0], x, old)
-
-
-def device_of(slot, nest):
-    return slot * 4 + lax.rem(2 * nest + 32 - slot // 8 - lax.rem(slot, 8), 4)
+    hit = jnp.concatenate([hit[:, :128], hit[:, 128:]], 0) > 0.5
+    scale = jnp.where(jnp.broadcast_to(count, (ROWS, 128)) == 2, 0.5, 1.0)
+    xs = []
+    for b in range(BINS):
+        got = placed[b * GY : (b + 1) * GY] + placed[(BINS + b) * GY : (BINS + b + 1) * GY]
+        xs.append(jnp.where(hit, jnp.concatenate([got[:, :128], got[:, 128:]], 0), field[b]))
+    xs = pick_each(xs, order)
+    for b in range(BINS):
+        x = advect(xs[b], scale * courant[0, b], col_shift)
+        xs[b] = advect(x, (scale * turn) * courant[1, b], row_shift)
+    xs = [x * sea for x in pick_each(xs, position)]
+    if number > 0:
+        still = jnp.broadcast_to(count, (ROWS, 128)) > number
+        xs = [jnp.where(still, x, field[b]) for b, x in enumerate(xs)]
+    return xs
 
 
 def step_kernel(
-    spectra, tables, wet, wind, send, recv, growth, dissipation, coupling, courant, count, result,
+    spectra, tables, wet, wind, send, recv, growth, dissipation, substeps, coupling, courant, result,
     field, lhs, wide, chosen, placed_at, going, coming, packed, windy,
     columns, coarse, grown, damped, weights, back,
     weight_sem, swap_send, swap_recv, own_sem, send_sem, recv_sem, back_send, back_recv,
+    plane_sem, all_sem,
 ):
     nest, me = lax.axis_index("nest"), lax.axis_index("bin")
-    slot = me // 4
-    integrates = device_of(slot, nest) == me
-    mine = jnp.where(integrates, 1, 0)
+    slot = lax.div(me, 4)
+    y, z, x_me = lax.div(me, 32), lax.rem(slot, 8), lax.rem(me, 4)
+    ys = [lax.rem(y + d, 4) for d in range(4)]
+    zs = [lax.rem(z + d, 8) for d in range(8)]
+    xs_at = [lax.rem(x_me + d, 4) for d in range(4)]
+
+    def integrator(dy, dz):
+        q = ys[dy] * 8 + zs[dz]
+        return q, q * 4 + lax.rem(2 * nest + 32 - ys[dy] - zs[dz], 4)
+
+    def peer(dy, dz, dx):
+        return ys[dy] * 32 + zs[dz] * 4 + xs_at[dx]
+
+    far = [0, 1, 2, 3, 4, 3, 2, 1]
+    near = [0, 1, 2, 1]
+    slots = sorted(
+        [(dy, dz) for dy in range(4) for dz in range(8)], key=lambda d: -(near[d[0]] + far[d[1]])
+    )[:-1]
+    sources = sorted(
+        [(dy, dz, dx) for dy in range(4) for dz in range(8) for dx in range(4)],
+        key=lambda d: -(near[d[0]] + far[d[1]] + near[d[2]]),
+    )[:-1]
+    own_device = integrator(0, 0)[1]
+    integrates = own_device == me
 
     def to(device):
         return {"bin": device}
 
-    def forward(q):
+    def forward(q, device):
         return pltpu.make_async_remote_copy(
             src_ref=packed.at[pl.ds(q * BINS, BINS)],
             dst_ref=columns.at[pl.ds(me * BINS, BINS)],
             send_sem=send_sem,
             recv_sem=recv_sem,
-            device_id=to(device_of(q, nest)),
+            device_id=to(device),
             device_id_type=pl.DeviceIdType.MESH,
         )
 
@@ -258,9 +302,6 @@
             columns.at[pl.ds(me * BINS, BINS)], back.at[pl.ds(slot * BINS, BINS)], own_sem
         )
 
-    def others(count, own):
-        return [lax.rem(own + i, count) for i in range(1, count)]
-
     def swap(number):
         return pltpu.make_async_remote_copy(
             src_ref=going.at[number],
@@ -271,17 +312,17 @@
             device_id_type=pl.DeviceIdType.MESH,
         )
 
+    def signal(semaphore, device):
+        pl.semaphore_signal(
+            semaphore, inc=1, device_id=device, device_id_type=pl.DeviceIdType.MESH
+        )
+
+    line_x = [to(peer(0, 0, d)) for d in range(1, 4)]
+    line_y = [to(peer(d, 0, 0)) for d in range(1, 4)]
+    line_z = [to(peer(0, d, 0)) for d in range(1, 8)]
     barrier = pltpu.get_barrier_semaphore()
-    pl.semaphore_signal(
-        barrier, inc=1, device_id={"nest": 1 - nest}, device_id_type=pl.DeviceIdType.MESH
-    )
-
-    @pl.when(integrates)
-    def _():
-        for s in others(SOURCES, me):
-            pl.semaphore_signal(
-                barrier, inc=1, device_id=to(s), device_id_type=pl.DeviceIdType.MESH
-            )
+    for device in line_z + line_y + line_x + [{"nest": 1 - nest}]:
+        signal(barrier, device)
 
     fetch = pltpu.make_async_copy(coupling, weights, weight_sem)
     fetch.start()
@@ -292,23 +333,28 @@
         x = load_split(spectra, b) * sea
         field[b] = x
         stage_rows(b, x, lhs)
-    chosen[...] = (iota((GX, NB), 0) == (send[...] & (GX - 1))).astype(f32).astype(bf16)
-    placed_at[...] = (iota((GX, NB), 0) == (recv[...] & (GX - 1))).astype(f32).astype(bf16)
+    chosen[...] = onehot(send[...] & (GX - 1))
+    placed_at[...] = onehot(recv[...] & (GX - 1))
     gather_send(send, chosen, lhs, going.at[0])
     order, position, turn = grid_order(tables)
     turn = jnp.concatenate([turn] * (ROWS // 8), 0)
 
-    pl.semaphore_wait(barrier, SLOTS - mine + 1)
+    pl.semaphore_wait(barrier, 14)
     swap(0).start()
+    for device in line_y:
+        signal(plane_sem, device)
     leave, enter, windy[...] = packing(wet_int, load_split(wind))
     swap(0).wait_recv()
 
+    count = substeps[...].reshape(1, 1)
     placed = receive(coming.at[0], recv, wide, placed_at)
-    for b in range(BINS):
-        x = substep(0, b, placed, field, courant, count, order, position, sea, turn)
+    for b, x in enumerate(substep(0, placed, field, courant, count, order, position, sea, turn)):
         field[b] = x
         stage_rows(b, x, lhs)
     gather_send(send, chosen, lhs, going.at[1])
+    pl.semaphore_wait(plane_sem, 3)
+    for device in line_z:
+        signal(all_sem, device)
     swap(1).start()
     for block in range(BINS):
         at = slice(block * 128, (block + 1) * 128)
@@ -317,19 +363,19 @@
     swap(1).wait_recv()
 
     placed = receive(coming.at[1], recv, wide, placed_at)
-    for b in range(BINS):
-        x = substep(1, b, placed, field, courant, count, order, position, sea, turn)
+    for b, x in enumerate(substep(1, placed, field, courant, count, order, position, sea, turn)):
         for k in range(STAGES):
             x = jnp.where(((enter >> k) & 1) == 1, linear_shift(x, 1 << k), x)
         packed[pl.ds(b, SLOTS, stride=BINS), :] = x[:SLOTS]
 
-    for q in others(SLOTS, slot):
-        forward(q).start()
+    pl.semaphore_wait(all_sem, 7)
+    for offset in slots:
+        forward(*integrator(*offset)).start()
     fetch.wait()
 
     @pl.when(jnp.logical_not(integrates))
     def _():
-        forward(slot).start()
+        forward(slot, own_device).start()
 
     @pl.when(integrates)
     def _():
@@ -349,8 +395,8 @@
             return carry
 
         lax.fori_loop(0, SRC, step, 0)
-        for s in others(SOURCES, me):
-            returning(s).start()
+        for offset in sources:
+            returning(peer(*offset)).start()
         own_out().start()
         own_out().wait()
         several(SLOTS - 1, back, back_send, back_recv).wait_recv()
@@ -359,13 +405,11 @@
     def _():
         several(SLOTS, back, back_send, back_recv).wait_recv()
 
-    wet_here = sea > 0.5
     for b in range(BINS):
         x = back[pl.ds(b, SLOTS, stride=BINS), :]
         x = jnp.concatenate([x, x], 0)
         for k in reversed(range(STAGES - 1)):
             x = jnp.where(((leave >> k) & 1) == 1, linear_unshift(x, 1 << k), x)
-        x = jnp.where(wet_here, x, 0.0)
         for half in range(2):
             result[b, pl.ds(half, GY, stride=2), :] = x[half * GY : (half + 1) * GY]
 
@@ -393,7 +437,7 @@
     result = pl.pallas_call(
         step_kernel,
         out_shape=jax.ShapeDtypeStruct((BINS, ROWS, 128), f32),
-        in_specs=[vmem] * 8 + [pl.BlockSpec(memory_space=pl.ANY), smem, smem],
+        in_specs=[vmem] * 9 + [pl.BlockSpec(memory_space=pl.ANY), smem],
         out_specs=vmem,
         scratch_shapes=[
             pltpu.VMEM((BINS, ROWS, 128), f32),
@@ -419,13 +463,16 @@
             pltpu.SemaphoreType.DMA,
             pltpu.SemaphoreType.DMA,
             pltpu.SemaphoreType.DMA,
+            pltpu.SemaphoreType.REGULAR,
+            pltpu.SemaphoreType.REGULAR,
         ],
         compiler_params=pltpu.CompilerParams(collective_id=0, has_side_effects=True),
     )(
         spectra.reshape(BINS, ROWS, 128), tables, wet_mask.reshape(plane), wind.reshape(plane),
-        send_list, recv_list, growth, dissipation, coupling,
-        courant, substep_count,
-    )
+        send_list, recv_list, growth, dissipation,
+        substep_count, coupling, courant,
+    )
+    result = jnp.where(wet_mask.reshape(plane)[None] == 1, result, 0.0)
     return result.reshape(1, BINS, ROWS * 128)
 
 

time: 48.4 us -> 43.8 us (0.905)
  Pallas kernels: 45.5 us -> 41 us
  other arithmetic: 0 us -> 1.71 us
  local copies, waits for them, and re-layouts: 1.69 us -> 0.01 us
    pallas_call x1, Pallas kernels: 45.5 us -> 41 us  [local(): pl.pallas_call(step_kernel, out_shape=jax.ShapeDtypeStruct((BINS, ROWS, 1...]
    select_n x0 -> x1, other arithmetic: none -> 1.7 us  [local(): result = jnp.where(wet_mask.reshape(plane)[None] == 1, result, 0.0)]
    unnamed x1 -> x2, local copies, waits for them, and re-layouts: 1.69 us -> 0.01 us
where the time goes in v3:
time: 43.8 us; the launch traced here: 43.4 us
  Pallas kernels  41 us (94%)
  other arithmetic  1.71 us (4%)
  between operations  0.68 us (2%)
    pallas_call x1, Pallas kernels, local(): pl.pallas_call(step_kernel, out_shape=jax.ShapeDtypeStruct((BINS, ROWS, 1...  41 us
    select_n x1, other arithmetic, local(): result = jnp.where(wet_mask.reshape(plane)[None] == 1, result, 0.0)  1.7 us

profile of v3, /device:TPU:2, one launch (start us, length us, event | category | flops | bytes accessed | tf_op | source)
XLA Modules:
  0.0 43.4 jit_solution(14221107907636341983)
XLA Ops:
  0.0 0.0 copy-start
  0.7 41.0 %shard_map.109 = f32[9,64,128]{2,1,0:T(8,128)} custom-call(f32[9,64,128]{2,1,0:T(8,128)} %bitcast.9, s32[256,128]{1,0:T(8,128)} %bitcast.12, s32[64,128]{1,0:T(8,128)} %bitcast.10, f32[64,128]{1,0:T(8,128)} %bitcast.13, s32[1,2048]{1,0:T(1,128)} %send.1, s32[1,2048]{1,0:T(1,128)} %recv.1, f32[1152]{0:T(1024)} %growth.1, f32[1152]{0:T(1024)} %dissipation.1, ...), custom_call_target="tpu_custom_call" | custom-call | tf_op jit(solution)/shard_map/pallas_call | solution.py:437
  41.7 0.0 copy-done
  41.7 1.7 %broadcast_select_fusion = f32[9,64,128]{2,1,0:T(8,128)} fusion(f32[9,64,128]{2,1,0:T(8,128)} %shard_map.109, pred[64,128]{1,0:T(8,128)(4,1)S(1)} %broadcast_compare_fusion), kind=kLoop, calls=%fused_computation | loop fusion | flops 73728 | bytes 598016 | tf_op jit(solution)/shard_map/jit(_where)/select_n | solution.py:475
  (1 shorter events, 0.0 us)
Async XLA Ops:
  0.0 41.7 %copy-start = (s32[1,8192]{1,0:T(1,128)S(1)}, s32[1,8192]{1,0:T(1,128)}, u32[]{:S(2)}) copy-start(s32[1,8192]{1,0:T(1,128)} %param.18) | copy-start | bytes 98308

commit v4 on v3

--- a/solution.py
+++ b/solution.py
@@ -15,9 +15,11 @@
 K = 1152
 ROWS = 64
 NB = 2048
+HALF = 1024
 SLOTS = 32
 SOURCES = 128
 STAGES = 13
+LANE_STAGES = 7
 f32, bf16, i32 = jnp.float32, jnp.bfloat16, jnp.int32
 
 
@@ -49,11 +51,26 @@
     return jnp.where(iota(x.shape, 1) >= 128 - amount, pltpu.roll(turned, ROWS - 1, 0), turned)
 
 
-def linear_unshift(x, amount):
-    if amount >= 128:
-        return pltpu.roll(x, amount // 128, 0)
-    turned = pltpu.roll(x, amount, 1)
-    return jnp.where(iota(x.shape, 1) < amount, pltpu.roll(turned, 1, 0), turned)
+def rows_unshift(x, amount):
+    return pltpu.roll(x, amount // 128, 0)
+
+
+def choose_each(firsts, seconds, lane, use_first):
+    parts = [[] for _ in firsts]
+    for at in range(0, ROWS, 8):
+        low = at % firsts[0].shape[0]
+        within, mask = lane[at : at + 8], use_first[at : at + 8]
+        for part, first, second in zip(parts, firsts, seconds):
+            part.append(
+                jnp.where(mask, lanes(first[low : low + 8], within), lanes(second[low : low + 8], within))
+            )
+    return [jnp.concatenate(part, 0) for part in parts]
+
+
+def pick_each(tables, index):
+    return choose_each(
+        [table[:GY] for table in tables], [table[GY:] for table in tables], index & 127, index < 128
+    )
 
 
 def col_shift(x, amount):
@@ -69,21 +86,24 @@
     return jnp.concatenate([pltpu.roll(x[:GY], turn, 0), pltpu.roll(x[GY:], turn, 0)], 0)
 
 
+def tall(x):
+    return jnp.concatenate([x] * (ROWS // 8), 0)
+
+
 def advect(field, rate, shift):
     magnitude = jnp.abs(rate)
     forward = rate >= 0.0
-    ahead = shift(field, 1)
-    upwind = jnp.where(forward, field, ahead)
-    downwind = jnp.where(forward, ahead, field)
-    far_upwind = jnp.where(forward, shift(field, -1), shift(field, 2))
-    estimate = (
-        0.5 * (upwind + downwind)
-        - 0.5 * magnitude * (downwind - upwind)
-        - ((1.0 - magnitude * magnitude) * (1.0 / 6.0)) * (downwind - 2.0 * upwind + far_upwind)
-    )
-    low, high = jnp.minimum(upwind, downwind), jnp.maximum(upwind, downwind)
-    face = jnp.minimum(jnp.maximum(estimate, low), high)
-    return field - rate * (face - shift(face, -1))
+    curve = (1.0 - magnitude * magnitude) * (1.0 / 6.0)
+    on_up, on_down = 0.5 + 0.5 * magnitude + 2.0 * curve, 0.5 - 0.5 * magnitude - curve
+    here, ahead = tall(jnp.where(forward, on_up, on_down)), tall(jnp.where(forward, on_down, on_up))
+    speed = tall(rate)
+    after = shift(field, 1)
+    far = jnp.where(speed >= 0.0, shift(field, -1), shift(field, 2))
+    estimate = here * field + ahead * after - tall(curve) * far
+    face = jnp.minimum(
+        jnp.maximum(estimate, jnp.minimum(field, after)), jnp.maximum(field, after)
+    )
+    return field - speed * (face - shift(face, -1))
 
 
 def onehot(within):
@@ -103,9 +123,9 @@
     lhs[(BINS + b) * GY : (BINS + b + 1) * GY, :] = rest
 
 
-def gather_send(send, chosen, lhs, out):
-    for c in range(NB // 256):
-        at = slice(c * 256, (c + 1) * 256)
+def gather_send(send, chosen, lhs, out, half):
+    for c in range(HALF // 256):
+        at = pl.ds(pl.multiple_of(half * HALF + c * 256, 256), 256)
         point = send[:, at]
         found = jnp.dot(lhs[...], chosen[:, at], preferred_element_type=f32)
         mine = iota((GY, 256), 0) == (point >> 8)
@@ -113,7 +133,7 @@
         for b in range(BINS):
             whole = found[b * GY : (b + 1) * GY] + found[(BINS + b) * GY : (BINS + b + 1) * GY]
             rows.append(jnp.sum(jnp.where(mine, whole, 0.0), axis=0, keepdims=True))
-        out[:, at] = jnp.concatenate(rows, 0)
+        out[:, c * 256 : (c + 1) * 256] = jnp.concatenate(rows, 0)
 
 
 def grid_order(tables):
@@ -161,76 +181,81 @@
         above_rows, rows.astype(bf16), preferred_element_type=f32
     )
     move = jnp.where(wet_int == 1, move.astype(i32), 0)
+    lane = iota((ROWS, 128), 1)
+    back_lane = lane - (move & 127)
     leave, enter = jnp.zeros((ROWS, 128), i32), jnp.zeros((ROWS, 128), i32)
     for k in range(STAGES):
+        if k == LANE_STAGES:
+            in_lane = lane + (move & 127)
         going = (move >> k) & 1
-        leave = leave | (going << k)
         other = linear_shift(move, 1 << k)
         coming = (other >> k) & 1
-        enter = enter | (coming << k)
+        leave, enter = leave | (going << k), enter | (coming << k)
         move = jnp.where(coming == 1, other, jnp.where(going == 1, 0, move))
-        windy = jnp.where(coming == 1, linear_shift(windy, 1 << k), windy)
-    return leave, enter, windy[:SLOTS]
-
-
-def receive(incoming, recv, lhs, rhs):
-    row = (recv[...] >> 8).astype(f32).astype(bf16)
-    mine = iota((GY, NB), 0).astype(f32).astype(bf16) == row
+    (windy,) = pack([windy], in_lane, enter)
+    return back_lane, leave, in_lane, enter, windy[:SLOTS]
+
+
+def pack(xs, in_lane, enter):
+    nexts = [pltpu.roll(x, ROWS - 1, 0) for x in xs]
+    xs = choose_each(xs, nexts, in_lane & 127, in_lane < 128)
+    for k in range(LANE_STAGES, STAGES):
+        coming = ((enter >> k) & 1) == 1
+        xs = [jnp.where(coming, linear_shift(x, 1 << k), x) for x in xs]
+    return xs
+
+
+def unpack(xs, back_lane, leave):
+    xs = [jnp.concatenate([x, x], 0) for x in xs]
+    for k in reversed(range(LANE_STAGES, STAGES - 1)):
+        going = ((leave >> k) & 1) == 1
+        xs = [jnp.where(going, rows_unshift(x, 1 << k), x) for x in xs]
+    previous = [pltpu.roll(x, 1, 0) for x in xs]
+    return choose_each(xs, previous, back_lane & 127, back_lane >= 0)
+
+
+def receive(incoming, recv, lhs, rhs, half):
+    at = pl.ds(pl.multiple_of(half * HALF, HALF), HALF)
+    row = (recv[:, at] >> 8).astype(f32).astype(bf16)
+    mine = iota((GY, HALF), 0).astype(f32).astype(bf16) == row
     zero = jnp.zeros((), bf16)
     for b in range(BINS):
         high, rest = two_parts(incoming[b : b + 1, :])
-        lhs[b * GY : (b + 1) * GY, :] = jnp.where(mine, jnp.broadcast_to(high, (GY, NB)), zero)
+        lhs[b * GY : (b + 1) * GY, :] = jnp.where(mine, jnp.broadcast_to(high, (GY, HALF)), zero)
         lhs[(BINS + b) * GY : (BINS + b + 1) * GY, :] = jnp.where(
-            mine, jnp.broadcast_to(rest, (GY, NB)), zero
+            mine, jnp.broadcast_to(rest, (GY, HALF)), zero
         )
     lhs[2 * BINS * GY :, :] = jnp.where(mine, jnp.ones((), bf16), zero)
     return lax.dot_general(
-        lhs[...], rhs[...], (((1,), (1,)), ((), ())), preferred_element_type=f32
-    )
-
-
-def pick_each(tables, index):
-    parts = [[] for _ in tables]
-    for at in range(0, ROWS, 8):
-        low = at % GY
-        here = index[at : at + 8]
-        within, first = here & 127, here < 128
-        for part, table in zip(parts, tables):
-            part.append(
-                jnp.where(
-                    first,
-                    lanes(table[low : low + 8], within),
-                    lanes(table[GY + low : GY + low + 8], within),
-                )
-            )
-    return [jnp.concatenate(part, 0) for part in parts]
+        lhs[...], rhs[:, at], (((1,), (1,)), ((), ())), preferred_element_type=f32
+    )
 
 
 def substep(number, placed, field, courant, count, order, position, sea, turn):
-    hit = placed[2 * BINS * GY :]
+    hit = placed[2 * BINS * GY :, :]
     hit = jnp.concatenate([hit[:, :128], hit[:, 128:]], 0) > 0.5
-    scale = jnp.where(jnp.broadcast_to(count, (ROWS, 128)) == 2, 0.5, 1.0)
+    scale = jnp.where(jnp.full((8, 128), count) == 2, 0.5, 1.0)
     xs = []
     for b in range(BINS):
-        got = placed[b * GY : (b + 1) * GY] + placed[(BINS + b) * GY : (BINS + b + 1) * GY]
+        got = placed[b * GY : (b + 1) * GY, :] + placed[(BINS + b) * GY : (BINS + b + 1) * GY, :]
         xs.append(jnp.where(hit, jnp.concatenate([got[:, :128], got[:, 128:]], 0), field[b]))
     xs = pick_each(xs, order)
     for b in range(BINS):
         x = advect(xs[b], scale * courant[0, b], col_shift)
         xs[b] = advect(x, (scale * turn) * courant[1, b], row_shift)
-    xs = [x * sea for x in pick_each(xs, position)]
+    xs = pick_each(xs, position)
     if number > 0:
-        still = jnp.broadcast_to(count, (ROWS, 128)) > number
-        xs = [jnp.where(still, x, field[b]) for b, x in enumerate(xs)]
-    return xs
+        still = jnp.full((ROWS, 128), count) > number
+        return [jnp.where(still, x, field[b]) for b, x in enumerate(xs)]
+    return [x * sea for x in xs]
 
 
 def step_kernel(
     spectra, tables, wet, wind, send, recv, growth, dissipation, substeps, coupling, courant, result,
-    field, lhs, wide, chosen, placed_at, going, coming, packed, windy,
+    field, lhs, wide, placed, chosen, placed_at, going, coming, packed, windy,
     columns, coarse, grown, damped, weights, back,
     weight_sem, swap_send, swap_recv, own_sem, send_sem, recv_sem, back_send, back_recv,
-    plane_sem, all_sem,
+    plane_sem, all_sem, counted, count_sem,
 ):
     nest, me = lax.axis_index("nest"), lax.axis_index("bin")
     slot = lax.div(me, 4)
@@ -312,6 +337,23 @@
             device_id_type=pl.DeviceIdType.MESH,
         )
 
+    def send_halves(number, start):
+        def half(i, carry):
+            gather_send(send, chosen, lhs, going.at[2 * number + i], i)
+            if start:
+                swap(2 * number + i).start()
+            return carry
+
+        lax.fori_loop(0, 2, half, 0)
+
+    def receive_halves(number):
+        def half(i, carry):
+            swap(2 * number + i).wait_recv()
+            placed[...] += receive(coming.at[2 * number + i], recv, wide, placed_at, i)
+            return carry
+
+        lax.fori_loop(0, 2, half, 0)
+
     def signal(semaphore, device):
         pl.semaphore_signal(
             semaphore, inc=1, device_id=device, device_id_type=pl.DeviceIdType.MESH
@@ -326,6 +368,8 @@
 
     fetch = pltpu.make_async_copy(coupling, weights, weight_sem)
     fetch.start()
+    fetch_count = pltpu.make_async_copy(substeps, counted, count_sem)
+    fetch_count.start()
 
     wet_int = load_split(wet)
     sea = wet_int.astype(f32)
@@ -335,37 +379,36 @@
         stage_rows(b, x, lhs)
     chosen[...] = onehot(send[...] & (GX - 1))
     placed_at[...] = onehot(recv[...] & (GX - 1))
-    gather_send(send, chosen, lhs, going.at[0])
+    send_halves(0, False)
     order, position, turn = grid_order(tables)
-    turn = jnp.concatenate([turn] * (ROWS // 8), 0)
+    fetch_count.wait()
+    count = counted[0]
 
     pl.semaphore_wait(barrier, 14)
     swap(0).start()
+    swap(1).start()
     for device in line_y:
         signal(plane_sem, device)
-    leave, enter, windy[...] = packing(wet_int, load_split(wind))
-    swap(0).wait_recv()
-
-    count = substeps[...].reshape(1, 1)
-    placed = receive(coming.at[0], recv, wide, placed_at)
-    for b, x in enumerate(substep(0, placed, field, courant, count, order, position, sea, turn)):
-        field[b] = x
-        stage_rows(b, x, lhs)
-    gather_send(send, chosen, lhs, going.at[1])
-    pl.semaphore_wait(plane_sem, 3)
-    for device in line_z:
-        signal(all_sem, device)
-    swap(1).start()
+    placed[...] = jnp.zeros_like(placed)
     for block in range(BINS):
         at = slice(block * 128, (block + 1) * 128)
         grown[at, :] = jnp.transpose(jnp.broadcast_to((SOURCE_DT * growth[at]).reshape(1, 128), (128, 128)))
         damped[at, :] = jnp.transpose(jnp.broadcast_to((SOURCE_DT * dissipation[at]).reshape(1, 128), (128, 128)))
-    swap(1).wait_recv()
-
-    placed = receive(coming.at[1], recv, wide, placed_at)
-    for b, x in enumerate(substep(1, placed, field, courant, count, order, position, sea, turn)):
-        for k in range(STAGES):
-            x = jnp.where(((enter >> k) & 1) == 1, linear_shift(x, 1 << k), x)
+
+    receive_halves(0)
+    for b, x in enumerate(substep(0, placed, field, courant, count, order, position, sea, turn)):
+        field[b] = x
+        stage_rows(b, x, lhs)
+    send_halves(1, True)
+    pl.semaphore_wait(plane_sem, 3)
+    for device in line_z:
+        signal(all_sem, device)
+    placed[...] = jnp.zeros_like(placed)
+    back_lane, leave, in_lane, enter, windy[...] = packing(wet_int, load_split(wind))
+
+    receive_halves(1)
+    xs = pack(substep(1, placed, field, courant, count, order, position, sea, turn), in_lane, enter)
+    for b, x in enumerate(xs):
         packed[pl.ds(b, SLOTS, stride=BINS), :] = x[:SLOTS]
 
     pl.semaphore_wait(all_sem, 7)
@@ -405,15 +448,14 @@
     def _():
         several(SLOTS, back, back_send, back_recv).wait_recv()
 
-    for b in range(BINS):
-        x = back[pl.ds(b, SLOTS, stride=BINS), :]
-        x = jnp.concatenate([x, x], 0)
-        for k in reversed(range(STAGES - 1)):
-            x = jnp.where(((leave >> k) & 1) == 1, linear_unshift(x, 1 << k), x)
+    xs = unpack(
+        [back[pl.ds(b, SLOTS, stride=BINS), :] for b in range(BINS)], back_lane, leave
+    )
+    for b, x in enumerate(xs):
         for half in range(2):
             result[b, pl.ds(half, GY, stride=2), :] = x[half * GY : (half + 1) * GY]
 
-    for number in range(SUBSTEPS):
+    for number in range(2 * SUBSTEPS):
         swap(number).wait_send()
 
     @pl.when(integrates)
@@ -436,17 +478,18 @@
     smem = pl.BlockSpec(memory_space=pltpu.SMEM)
     result = pl.pallas_call(
         step_kernel,
-        out_shape=jax.ShapeDtypeStruct((BINS, ROWS, 128), f32),
-        in_specs=[vmem] * 9 + [pl.BlockSpec(memory_space=pl.ANY), smem],
+        out_shape=pltpu.VMEM((BINS, ROWS, 128), f32),
+        in_specs=[vmem] * 8 + [pl.BlockSpec(memory_space=pl.ANY)] * 2 + [smem],
         out_specs=vmem,
         scratch_shapes=[
             pltpu.VMEM((BINS, ROWS, 128), f32),
             pltpu.VMEM((2 * BINS * GY, GX), bf16),
-            pltpu.VMEM((2 * BINS * GY + GY, NB), bf16),
+            pltpu.VMEM((2 * BINS * GY + GY, HALF), bf16),
+            pltpu.VMEM((2 * BINS * GY + GY, GX), f32),
             pltpu.VMEM((GX, NB), bf16),
             pltpu.VMEM((GX, NB), bf16),
-            pltpu.VMEM((SUBSTEPS, BINS, NB), f32),
-            pltpu.VMEM((SUBSTEPS, BINS, NB), f32),
+            pltpu.VMEM((2 * SUBSTEPS, BINS, HALF), f32),
+            pltpu.VMEM((2 * SUBSTEPS, BINS, HALF), f32),
             pltpu.VMEM((SLOTS * BINS, 128), f32),
             pltpu.VMEM((SLOTS, 128), f32),
             pltpu.VMEM((K, 128), f32),
@@ -456,8 +499,8 @@
             pltpu.VMEM((K, K), bf16),
             pltpu.VMEM((SLOTS * BINS, 128), f32),
             pltpu.SemaphoreType.DMA,
-            pltpu.SemaphoreType.DMA((SUBSTEPS,)),
-            pltpu.SemaphoreType.DMA((SUBSTEPS,)),
+            pltpu.SemaphoreType.DMA((2 * SUBSTEPS,)),
+            pltpu.SemaphoreType.DMA((2 * SUBSTEPS,)),
             pltpu.SemaphoreType.DMA,
             pltpu.SemaphoreType.DMA,
             pltpu.SemaphoreType.DMA,
@@ -465,6 +508,8 @@
             pltpu.SemaphoreType.DMA,
             pltpu.SemaphoreType.REGULAR,
             pltpu.SemaphoreType.REGULAR,
+            pltpu.SMEM((1,), i32),
+            pltpu.SemaphoreType.DMA,
         ],
         compiler_params=pltpu.CompilerParams(collective_id=0, has_side_effects=True),
     )(

time: 43.8 us -> 41.8 us (0.954)
  Pallas kernels: 41 us -> 39.7 us
  other arithmetic: 1.71 us -> 0.75 us
    pallas_call x1, Pallas kernels: 41 us -> 39.7 us  [local(): pl.pallas_call(step_kernel, out_shape=pltpu.VMEM((BINS, ROWS, 128), f32),...]
    select_n x1, other arithmetic: 1.7 us -> 0.74 us  [local(): result = jnp.where(wet_mask.reshape(plane)[None] == 1, result, 0.0)]
where the time goes in v4:
time: 41.8 us; the launch traced here: 41.1 us
  Pallas kernels  39.7 us (95%)
  other arithmetic  0.75 us (2%)
  between operations  0.68 us (2%)
    pallas_call x1, Pallas kernels, local(): pl.pallas_call(step_kernel, out_shape=pltpu.VMEM((BINS, ROWS, 128), f32),...  39.7 us

profile of v4, /device:TPU:2, one launch (start us, length us, event | category | flops | bytes accessed | tf_op | source)
XLA Modules:
  0.0 41.1 jit_solution(16879976187613028228)
XLA Ops:
  0.0 0.0 copy-start
  0.7 39.7 %shard_map.109 = f32[9,64,128]{2,1,0:T(8,128)S(1)} custom-call(f32[9,64,128]{2,1,0:T(8,128)} %bitcast.9, s32[256,128]{1,0:T(8,128)} %bitcast.12, s32[64,128]{1,0:T(8,128)} %bitcast.10, f32[64,128]{1,0:T(8,128)} %bitcast.13, s32[1,2048]{1,0:T(1,128)} %send.1, s32[1,2048]{1,0:T(1,128)} %recv.1, f32[1152]{0:T(1024)} %growth.1, f32[1152]{0:T(1024)} %dissipation.1, ...), custom_call_target="tpu_custom_call" | custom-call | tf_op jit(solution)/shard_map/pallas_call | solution.py:479
  40.4 0.0 copy-done
  40.4 0.7 %broadcast_select_fusion = f32[9,64,128]{2,1,0:T(8,128)} fusion(f32[9,64,128]{2,1,0:T(8,128)S(1)} %shard_map.109, pred[64,128]{1,0:T(8,128)(4,1)S(1)} %broadcast_compare_fusion), kind=kLoop, calls=%fused_computation | loop fusion | flops 73728 | bytes 598016 | tf_op jit(solution)/shard_map/jit(_where)/select_n | solution.py:520
  (1 shorter events, 0.0 us)
Async XLA Ops:
  0.0 40.4 %copy-start = (s32[1,8192]{1,0:T(1,128)S(1)}, s32[1,8192]{1,0:T(1,128)}, u32[]{:S(2)}) copy-start(s32[1,8192]{1,0:T(1,128)} %param.18) | copy-start | bytes 98308

commit v5 on v4

--- a/solution.py
+++ b/solution.py
@@ -214,20 +214,20 @@
     return choose_each(xs, previous, back_lane & 127, back_lane >= 0)
 
 
-def receive(incoming, recv, lhs, rhs, half):
-    at = pl.ds(pl.multiple_of(half * HALF, HALF), HALF)
-    row = (recv[:, at] >> 8).astype(f32).astype(bf16)
-    mine = iota((GY, HALF), 0).astype(f32).astype(bf16) == row
+def receive(incoming, recv, lhs, rhs):
+    row = (recv[...] >> 8).astype(f32).astype(bf16)
+    mine = iota((GY, NB), 0).astype(f32).astype(bf16) == row
     zero = jnp.zeros((), bf16)
     for b in range(BINS):
-        high, rest = two_parts(incoming[b : b + 1, :])
-        lhs[b * GY : (b + 1) * GY, :] = jnp.where(mine, jnp.broadcast_to(high, (GY, HALF)), zero)
+        value = jnp.concatenate([incoming[half, b : b + 1, :] for half in range(2)], 1)
+        high, rest = two_parts(value)
+        lhs[b * GY : (b + 1) * GY, :] = jnp.where(mine, jnp.broadcast_to(high, (GY, NB)), zero)
         lhs[(BINS + b) * GY : (BINS + b + 1) * GY, :] = jnp.where(
-            mine, jnp.broadcast_to(rest, (GY, HALF)), zero
+            mine, jnp.broadcast_to(rest, (GY, NB)), zero
         )
     lhs[2 * BINS * GY :, :] = jnp.where(mine, jnp.ones((), bf16), zero)
     return lax.dot_general(
-        lhs[...], rhs[:, at], (((1,), (1,)), ((), ())), preferred_element_type=f32
+        lhs[...], rhs[...], (((1,), (1,)), ((), ())), preferred_element_type=f32
     )
 
 
@@ -252,7 +252,7 @@
 
 def step_kernel(
     spectra, tables, wet, wind, send, recv, growth, dissipation, substeps, coupling, courant, result,
-    field, lhs, wide, placed, chosen, placed_at, going, coming, packed, windy,
+    field, lhs, wide, chosen, placed_at, going, coming, packed, windy,
     columns, coarse, grown, damped, weights, back,
     weight_sem, swap_send, swap_recv, own_sem, send_sem, recv_sem, back_send, back_recv,
     plane_sem, all_sem, counted, count_sem,
@@ -347,12 +347,9 @@
         lax.fori_loop(0, 2, half, 0)
 
     def receive_halves(number):
-        def half(i, carry):
-            swap(2 * number + i).wait_recv()
-            placed[...] += receive(coming.at[2 * number + i], recv, wide, placed_at, i)
-            return carry
-
-        lax.fori_loop(0, 2, half, 0)
+        for half in range(2):
+            swap(2 * number + half).wait_recv()
+        return receive(coming.at[2 * number : 2 * number + 2], recv, wide, placed_at)
 
     def signal(semaphore, device):
         pl.semaphore_signal(
@@ -389,13 +386,12 @@
     swap(1).start()
     for device in line_y:
         signal(plane_sem, device)
-    placed[...] = jnp.zeros_like(placed)
     for block in range(BINS):
         at = slice(block * 128, (block + 1) * 128)
         grown[at, :] = jnp.transpose(jnp.broadcast_to((SOURCE_DT * growth[at]).reshape(1, 128), (128, 128)))
         damped[at, :] = jnp.transpose(jnp.broadcast_to((SOURCE_DT * dissipation[at]).reshape(1, 128), (128, 128)))
 
-    receive_halves(0)
+    placed = receive_halves(0)
     for b, x in enumerate(substep(0, placed, field, courant, count, order, position, sea, turn)):
         field[b] = x
         stage_rows(b, x, lhs)
@@ -403,10 +399,9 @@
     pl.semaphore_wait(plane_sem, 3)
     for device in line_z:
         signal(all_sem, device)
-    placed[...] = jnp.zeros_like(placed)
     back_lane, leave, in_lane, enter, windy[...] = packing(wet_int, load_split(wind))
 
-    receive_halves(1)
+    placed = receive_halves(1)
     xs = pack(substep(1, placed, field, courant, count, order, position, sea, turn), in_lane, enter)
     for b, x in enumerate(xs):
         packed[pl.ds(b, SLOTS, stride=BINS), :] = x[:SLOTS]
@@ -484,8 +479,7 @@
         scratch_shapes=[
             pltpu.VMEM((BINS, ROWS, 128), f32),
             pltpu.VMEM((2 * BINS * GY, GX), bf16),
-            pltpu.VMEM((2 * BINS * GY + GY, HALF), bf16),
-            pltpu.VMEM((2 * BINS * GY + GY, GX), f32),
+            pltpu.VMEM((2 * BINS * GY + GY, NB), bf16),
             pltpu.VMEM((GX, NB), bf16),
             pltpu.VMEM((GX, NB), bf16),
             pltpu.VMEM((2 * SUBSTEPS, BINS, HALF), f32),

time: 41.8 us -> 39.7 us (0.950); the launches traced: 41.1 us -> 39.6 us
  Pallas kernels: 39.7 us -> 38.1 us
    pallas_call x1, Pallas kernels: 39.7 us -> 38.1 us  [local(): pl.pallas_call(step_kernel, out_shape=pltpu.VMEM((BINS, ROWS, 128), f32),...]
where the time goes in v5:
time: 39.7 us; the launch traced here: 39.6 us
  Pallas kernels  38.1 us (96%)
  other arithmetic  0.75 us (2%)
  between operations  0.68 us (2%)
    pallas_call x1, Pallas kernels, local(): pl.pallas_call(step_kernel, out_shape=pltpu.VMEM((BINS, ROWS, 128), f32),...  38.1 us

profile of v5, /device:TPU:2, one launch (start us, length us, event | category | flops | bytes accessed | tf_op | source)
XLA Modules:
  0.0 39.6 jit_solution(9521722184862340229)
XLA Ops:
  0.0 0.0 copy-start
  0.7 38.1 %shard_map.109 = f32[9,64,128]{2,1,0:T(8,128)S(1)} custom-call(f32[9,64,128]{2,1,0:T(8,128)} %bitcast.9, s32[256,128]{1,0:T(8,128)} %bitcast.12, s32[64,128]{1,0:T(8,128)} %bitcast.10, f32[64,128]{1,0:T(8,128)} %bitcast.13, s32[1,2048]{1,0:T(1,128)} %send.1, s32[1,2048]{1,0:T(1,128)} %recv.1, f32[1152]{0:T(1024)} %growth.1, f32[1152]{0:T(1024)} %dissipation.1, ...), custom_call_target="tpu_custom_call" | custom-call | tf_op jit(solution)/shard_map/pallas_call | solution.py:474
  38.8 0.0 copy-done
  38.8 0.7 %broadcast_select_fusion = f32[9,64,128]{2,1,0:T(8,128)} fusion(f32[9,64,128]{2,1,0:T(8,128)S(1)} %shard_map.109, pred[64,128]{1,0:T(8,128)(4,1)S(1)} %broadcast_compare_fusion), kind=kLoop, calls=%fused_computation | loop fusion | flops 73728 | bytes 598016 | tf_op jit(solution)/shard_map/jit(_where)/select_n | solution.py:514
  (1 shorter events, 0.0 us)
Async XLA Ops:
  0.0 38.8 %copy-start = (s32[1,8192]{1,0:T(1,128)S(1)}, s32[1,8192]{1,0:T(1,128)}, u32[]{:S(2)}) copy-start(s32[1,8192]{1,0:T(1,128)} %param.18) | copy-start | bytes 98308

commit v6 on v5

--- a/solution.py
+++ b/solution.py
@@ -378,6 +378,7 @@
     placed_at[...] = onehot(recv[...] & (GX - 1))
     send_halves(0, False)
     order, position, turn = grid_order(tables)
+    back_lane, leave, in_lane, enter, windy[...] = packing(wet_int, load_split(wind))
     fetch_count.wait()
     count = counted[0]
 
@@ -386,11 +387,6 @@
     swap(1).start()
     for device in line_y:
         signal(plane_sem, device)
-    for block in range(BINS):
-        at = slice(block * 128, (block + 1) * 128)
-        grown[at, :] = jnp.transpose(jnp.broadcast_to((SOURCE_DT * growth[at]).reshape(1, 128), (128, 128)))
-        damped[at, :] = jnp.transpose(jnp.broadcast_to((SOURCE_DT * dissipation[at]).reshape(1, 128), (128, 128)))
-
     placed = receive_halves(0)
     for b, x in enumerate(substep(0, placed, field, courant, count, order, position, sea, turn)):
         field[b] = x
@@ -399,7 +395,10 @@
     pl.semaphore_wait(plane_sem, 3)
     for device in line_z:
         signal(all_sem, device)
-    back_lane, leave, in_lane, enter, windy[...] = packing(wet_int, load_split(wind))
+    for block in range(BINS):
+        at = slice(block * 128, (block + 1) * 128)
+        grown[at, :] = jnp.transpose(jnp.broadcast_to((SOURCE_DT * growth[at]).reshape(1, 128), (128, 128)))
+        damped[at, :] = jnp.transpose(jnp.broadcast_to((SOURCE_DT * dissipation[at]).reshape(1, 128), (128, 128)))
 
     placed = receive_halves(1)
     xs = pack(substep(1, placed, field, courant, count, order, position, sea, turn), in_lane, enter)

time: 39.7 us -> 39.7 us (level)
  no operation moved by 1% of the time
where the time goes in v6:
time: 39.7 us; the launch traced here: 39.6 us
  Pallas kernels  38.2 us (96%)
  other arithmetic  0.75 us (2%)
  between operations  0.68 us (2%)
    pallas_call x1, Pallas kernels, local(): pl.pallas_call(step_kernel, out_shape=pltpu.VMEM((BINS, ROWS, 128), f32),...  38.2 us

profile of v6, /device:TPU:2, one launch (start us, length us, event | category | flops | bytes accessed | tf_op | source)
XLA Modules:
  0.0 39.6 jit_solution(17217030667852389097)
XLA Ops:
  0.0 0.0 copy-start
  0.7 38.2 %shard_map.109 = f32[9,64,128]{2,1,0:T(8,128)S(1)} custom-call(f32[9,64,128]{2,1,0:T(8,128)} %bitcast.9, s32[256,128]{1,0:T(8,128)} %bitcast.12, s32[64,128]{1,0:T(8,128)} %bitcast.10, f32[64,128]{1,0:T(8,128)} %bitcast.13, s32[1,2048]{1,0:T(1,128)} %send.1, s32[1,2048]{1,0:T(1,128)} %recv.1, f32[1152]{0:T(1024)} %growth.1, f32[1152]{0:T(1024)} %dissipation.1, ...), custom_call_target="tpu_custom_call" | custom-call | tf_op jit(solution)/shard_map/pallas_call | solution.py:473
  38.8 0.0 copy-done
  38.8 0.7 %broadcast_select_fusion = f32[9,64,128]{2,1,0:T(8,128)} fusion(f32[9,64,128]{2,1,0:T(8,128)S(1)} %shard_map.109, pred[64,128]{1,0:T(8,128)(4,1)S(1)} %broadcast_compare_fusion), kind=kLoop, calls=%fused_computation | loop fusion | flops 73728 | bytes 598016 | tf_op jit(solution)/shard_map/jit(_where)/select_n | solution.py:513
  (1 shorter events, 0.0 us)
Async XLA Ops:
  0.0 38.8 %copy-start = (s32[1,8192]{1,0:T(1,128)S(1)}, s32[1,8192]{1,0:T(1,128)}, u32[]{:S(2)}) copy-start(s32[1,8192]{1,0:T(1,128)} %param.18) | copy-start | bytes 98308
